TPU v7x, 32 devices: a whole 2x2x4 slice. The times are simulated.
32 devices in a mesh: tile: 4 (over y, core), tm: 8 (over z, x).
Axes of the slice: x: 2, y: 2, z: 4, core: 2. Of those that a mesh axis runs over, the one named last changes fastest.
Arguments:
- pixels: bfloat16 [192, 16, 64, 256], P(('tile', 'tm')), may hold values from -6 to 6
- slot_tile: int32 [192], replicated, may hold values from -1 to 95, as said below
- w_space: bfloat16 [3, 3, 256, 512], replicated, may hold values from -0.125 to 0.125
- b_space: float32 [512], replicated, may hold values from -3 to 3
- w_time: bfloat16 [3, 512, 512], replicated, may hold values from -0.15625 to 0.15625
- b_time: float32 [512], replicated, may hold values from -3 to 3
- gain: float32 [512], replicated, may hold values from 0.1 to 1.9
Outputs:
- latent: bfloat16 [96, 16, 16, 512], P('tile', 'tm')
Inputs may be any that keep to these rules, and one draw needn't show every extreme that they name: `slot_tile`: every tile id 0..95 stands in exactly one slot, -1 marks an empty slot. On each device (the 6 slots of one device in order) the live slots come first; the devices form aligned blocks of four consecutive devices whose live slots number 2 * 3, 3, 3 and 0 in some order. A group is 24 consecutive tile ids (tile id // 24); at most 2 slots of one device hold tiles of one group, and some device holds exactly 2 of one group.
All inputs are finite; a program needn't handle non-finite values.
Results may differ from a plain program's by a relative error of at most 0.0044.
Values may be sent and summed in bfloat16 or wider, within the bound.
A program may use at most 64 MiB of HBM per device.

v0:
```python
import functools

import jax
import jax.numpy as jnp
from jax import lax
from jax.experimental import pallas as pl
from jax.experimental.pallas import tpu as pltpu
from jax.sharding import PartitionSpec as P

TILE_SIDE = 8


def conv_space(raw_tiles, w_space, b_space):
    number, frames, pix_count, channels = raw_tiles.shape
    grid = raw_tiles.reshape(number * frames, TILE_SIDE, TILE_SIDE, channels)
    total = lax.conv_general_dilated(
        grid,
        w_space,
        (2, 2),
        ((1, 1), (1, 1)),
        dimension_numbers=("NHWC", "HWIO", "NHWC"),
        preferred_element_type=jnp.float32,
    )
    active = jax.nn.silu(total + b_space)
    half_side = TILE_SIDE // 2
    return active.astype(jnp.bfloat16).reshape(number, frames, half_side * half_side, -1)


def tables(slot_tile, rows, groups, bucket, group_tiles, my_row):
    table = slot_tile.reshape(rows, -1)
    width = table.shape[1]
    group_of = jnp.where(table >= 0, lax.div(table, group_tiles), groups)
    pos = jnp.arange(width, dtype=jnp.int32)
    earlier = pos[None, :] < pos[:, None]
    same = (group_of[:, :, None] == group_of[:, None, :]) & earlier[None]
    rank = jnp.sum(same.astype(jnp.int32), axis=2)
    target = group_of * bucket + rank
    own_target = lax.dynamic_index_in_dim(target, my_row, 0, keepdims=False)
    own_live = lax.dynamic_index_in_dim(table, my_row, 0, keepdims=False) >= 0
    own_target = jnp.where(own_live, own_target, -1)
    places = jnp.arange(groups * bucket, dtype=jnp.int32)
    send_idx = jnp.sum(
        jnp.where(own_target[None, :] == places[:, None], pos[None, :], 0), axis=1
    )
    wanted = my_row * group_tiles + jnp.arange(group_tiles, dtype=jnp.int32)
    arrived = jnp.arange(rows, dtype=jnp.int32)[:, None] * bucket + rank
    pick_idx = jnp.sum(
        jnp.where(
            table.reshape(-1)[None, :] == wanted[:, None], arrived.reshape(-1)[None, :], 0
        ),
        axis=1,
    )
    return send_idx, pick_idx


def kernel(
    rows, slabs, cap, bucket, group_tiles,
    send_idx, pick_idx, src, w_time, b_time, gain, out,
    got1a, got1b, out2, got2a, got2b, feats, halo, total,
    send1, recv1, send2, recv2, send3, recv3,
):
    frames = 2
    got1, got2 = (got1a, got1b), (got2a, got2b)
    row = lax.axis_index("tile")
    slab = lax.axis_index("tm")
    barrier = pltpu.get_barrier_semaphore()
    for k in range(1, slabs):
        pl.semaphore_signal(barrier, inc=1, device_id={"tm": lax.rem(slab + k, slabs)})
    for k in range(1, rows):
        pl.semaphore_signal(barrier, inc=1, device_id={"tile": lax.rem(row + k, rows)})
    pl.semaphore_wait(barrier, slabs + rows - 2)

    def copy1(f, k):
        to = lax.rem(slab + k, slabs)
        return pltpu.make_async_remote_copy(
            src_ref=src.at[:, to * frames + f],
            dst_ref=got1[f].at[pl.ds(slab * cap, cap)],
            send_sem=send1.at[f, k - 1],
            recv_sem=recv1.at[f, k - 1],
            device_id={"tm": to},
        )

    def copy2(f, k):
        to = lax.rem(row + k, rows)
        return pltpu.make_async_remote_copy(
            src_ref=out2.at[f, pl.ds(to * bucket, bucket)],
            dst_ref=got2[f].at[pl.ds(row * bucket, bucket)],
            send_sem=send2.at[f, k - 1],
            recv_sem=recv2.at[f, k - 1],
            device_id={"tile": to},
        )

    def copy3(f):
        return pltpu.make_async_remote_copy(
            src_ref=feats.at[f],
            dst_ref=halo.at[f],
            send_sem=send3.at[f],
            recv_sem=recv3.at[f],
            device_id={"tm": lax.rem(slab + 1, slabs)},
        )

    for f in range(frames):
        for k in range(1, slabs):
            copy1(f, k).start()
    for f in range(frames):
        got1[f][pl.ds(slab * cap, cap)] = src[:, slab * frames + f]
        for k in range(1, slabs):
            copy1(f, k).wait_recv()

        @pl.loop(0, rows * bucket)
        def _(i):
            out2[f, i] = got1[f][send_idx[i]]

        for k in range(1, rows):
            copy2(f, k).start()

        @pl.loop(0, bucket)
        def _(j):
            got2[f][row * bucket + j] = got1[f][send_idx[row * bucket + j]]

        for k in range(1, rows):
            copy2(f, k).wait_recv()

        @pl.loop(0, group_tiles)
        def _(i):
            feats[f, i] = got2[f][pick_idx[i]]

        @pl.when(slab < slabs - 1)
        def _():
            copy3(f).start()

    part = group_tiles // 2
    height = part * 16

    def flat(value):
        return value.reshape(height, value.shape[-1])

    @pl.loop(0, 2)
    def _(c):
        at = pl.ds(c * part, part)
        own = [flat(feats[0, at]), flat(feats[1, at])]
        for f in range(frames):
            mixed = own[f].astype(jnp.float32) + b_time[...]
            for lag in range(f + 1):
                mixed = mixed + jnp.dot(
                    own[f - lag], w_time[lag], preferred_element_type=jnp.float32
                )
            total[f, c] = mixed

    for f in range(frames):

        @pl.when(slab > 0)
        def _():
            copy3(f).wait_recv()

        @pl.when(slab == 0)
        def _():
            halo[f] = jnp.zeros(halo.shape[1:], halo.dtype)

    @pl.loop(0, 2)
    def _(c):
        at = pl.ds(c * part, part)
        before = [flat(halo[0, at]), flat(halo[1, at])]
        for f in range(frames):
            mixed = total[f, c]
            for lag in range(f + 1, 3):
                mixed = mixed + jnp.dot(
                    before[2 + f - lag], w_time[lag], preferred_element_type=jnp.float32
                )
            scale = lax.rsqrt(jnp.mean(mixed * mixed, axis=-1, keepdims=True) + 1e-06)
            value = (mixed * scale * gain[...]).astype(jnp.bfloat16)
            out[at, f] = value.reshape(part, 16, value.shape[-1])

    for f in range(frames):
        for k in range(1, slabs):
            copy1(f, k).wait_send()
        for k in range(1, rows):
            copy2(f, k).wait_send()

        @pl.when(slab < slabs - 1)
        def _():
            copy3(f).wait_send()


def body(rows, slabs, pixels, slot_tile, w_space, b_space, w_time, b_time, gain):
    cap, all_frames = pixels.shape[:2]
    channels = w_space.shape[-1]
    group_tiles = cap // 2 * slabs
    per_group = (cap + rows - 1) // rows
    bucket = per_group * 3 * (slabs // 4)
    frames = all_frames // slabs
    send_idx, pick_idx = tables(
        slot_tile, rows, rows, bucket, group_tiles, lax.axis_index("tile")
    )
    spatial = conv_space(pixels, w_space, b_space)
    vmem = pl.BlockSpec(memory_space=pltpu.VMEM)
    smem = pl.BlockSpec(memory_space=pltpu.SMEM)
    bf16 = jnp.bfloat16
    dma = pltpu.SemaphoreType.DMA
    return pl.pallas_call(
        functools.partial(kernel, rows, slabs, cap, bucket, group_tiles),
        out_shape=jax.ShapeDtypeStruct((group_tiles, frames, 16, channels), bf16),
        in_specs=[smem, smem, vmem, vmem, vmem, vmem],
        out_specs=vmem,
        scratch_shapes=[
            pltpu.VMEM((slabs * cap, 16, channels), bf16),
            pltpu.VMEM((slabs * cap, 16, channels), bf16),
            pltpu.VMEM((frames, rows * bucket, 16, channels), bf16),
            pltpu.VMEM((rows * bucket, 16, channels), bf16),
            pltpu.VMEM((rows * bucket, 16, channels), bf16),
            pltpu.VMEM((frames, group_tiles, 16, channels), bf16),
            pltpu.VMEM((frames, group_tiles, 16, channels), bf16),
            pltpu.VMEM((frames, 2, group_tiles * 8, channels), jnp.float32),
            dma((frames, slabs - 1)),
            dma((frames, slabs - 1)),
            dma((frames, rows - 1)),
            dma((frames, rows - 1)),
            dma((frames,)),
            dma((frames,)),
        ],
        compiler_params=pltpu.CompilerParams(collective_id=0, has_side_effects=True),
    )(send_idx, pick_idx, spatial, w_time, b_time[None], gain[None])


def solution(mesh):
    return jax.shard_map(
        functools.partial(body, mesh.shape["tile"], mesh.shape["tm"]),
        mesh=mesh,
        in_specs=(P(("tile", "tm"), None, None, None), P(), P(), P(), P(), P(), P()),
        out_specs=P("tile", "tm", None, None),
        check_vma=False,
    )
```

profile of v0, /device:TPU:21, one launch (start us, length us, event | category | flops | bytes accessed | tf_op | source)
XLA Modules:
  0.0 77.1 jit_solution(17176763309595155135)
XLA Ops:
  0.0 0.0 copy-start
  0.0 0.9 %reshape.64 = s32[4,48]{1,0:T(4,128)S(1)} reshape(s32[192]{0:T(256)} %param.8) | data formatting | bytes 1536 | tf_op jit(solution)/shard_map/reshape | solution.py:30
  1.0 0.2 convert_reduce_fusion
  1.2 0.1 broadcast_add_fusion
  1.3 0.1 add.51
  1.3 1.4 %select_reduce_fusion.pick_idx = s32[24]{0:T(128)} fusion(s32[192]{0:T(256)S(1)} %add.51, s32[192]{0:T(256)} %param.8, s32[24]{0:T(128)S(1)} %iota_add_fusion), kind=kLoop, calls=%fused_computation.4 | loop fusion | flops 13800 | bytes 1728 | tf_op jit(solution)/shard_map/reduce_sum | solution.py:47
  2.7 0.6 select_reduce_fusion.1.send_idx
  3.3 0.0 copy-done
  3.3 6.6 %multiply_convert_fusion = bf16[96,4,4,512]{3,0,2,1:T(8,128)(2,1)S(1)} fusion(bf16[3,3,256,512]{3,2,1,0:T(8,128)(2,1)S(1)} %copy-done, bf16[96,8,8,256]{3,2,1,0:T(8,128)(2,1)} %bitcast.10, f32[512]{0:T(512)} %param.10), kind=kOutput, calls=%fused_computation.2 | convolution fusion | flops 3049783296 | bytes 7079936 | tf_op jit(solution)/shard_map/conv_general_dilated | solution.py:16
  9.9 2.1 %copy.12.src = bf16[6,16,16,512]{3,2,1,0:T(8,128)(2,1)} copy(bf16[6,16,16,512]{3,1,0,2:T(8,128)(2,1)S(1)} %bitcast.7) | data formatting | bytes 3145728 | tf_op jit(solution)/shard_map/reshape | solution.py:26
  12.0 63.0 %shard_map.73 = bf16[24,2,16,512]{3,2,1,0:T(8,128)(2,1)} custom-call(s32[48]{0:T(128)} %select_reduce_fusion.1.send_idx, s32[24]{0:T(128)} %select_reduce_fusion.pick_idx, bf16[6,16,16,512]{3,2,1,0:T(8,128)(2,1)} %copy.12.src, bf16[3,512,512]{2,1,0:T(8,128)(2,1)} %w_time.1, f32[1,512]{1,0:T(1,128)} %bitcast.8, f32[1,512]{1,0:T(1,128)} %bitcast.9), custom_call_target="tpu_custom_call" | custom-call | tf_op jit(solution)/shard_map/pallas_call | solution.py:200
  75.0 2.1 %copy.18 = bf16[24,2,16,512]{3,2,1,0:T(8,128)(2,1)} copy(bf16[24,2,16,512]{3,2,1,0:T(8,128)(2,1)} %shard_map.73) | data formatting | bytes 1572864
  (5 shorter events, 0.0 us)
Async XLA Ops:
  0.0 3.3 %copy-start = (bf16[3,3,256,512]{3,2,1,0:T(8,128)(2,1)S(1)}, bf16[3,3,256,512]{3,2,1,0:T(8,128)(2,1)}, u32[]{:S(2)}) copy-start(bf16[3,3,256,512]{3,2,1,0:T(8,128)(2,1)} %param.9) | copy-start | bytes 7077892
where the time goes:
time: 77.3 us; the launch traced here: 77.1 us
  Pallas kernels  63 us (82%)
  matrix products  6.59 us (9%)
  local copies, waits for them, and re-layouts  5.14 us (7%)
  other arithmetic  2.32 us (3%)
    pallas_call x1, Pallas kernels, body(): pl.pallas_call(functools.partial(kernel, rows, slabs, cap, bucket, group_...  63 us
    conv_general_dilated x1, matrix products, conv_space(): lax.conv_general_dilated(grid, w_space, (2, 2), ((1, 1), (1, 1)), dimensi...  6.59 us
    unnamed x3, local copies, waits for them, and re-layouts  2.09 us
    reshape x1, local copies, waits for them, and re-layouts, conv_space(): active.astype(jnp.bfloat16)  2.05 us

commit v1 on v0

--- a/solution.py
+++ b/solution.py
@@ -8,6 +8,8 @@
 from jax.sharding import PartitionSpec as P
 
 TILE_SIDE = 8
+HALF = 4
+BASE = 3
 
 
 def conv_space(raw_tiles, w_space, b_space):
@@ -222,9 +224,376 @@
     )(send_idx, pick_idx, spatial, w_time, b_time[None], gain[None])
 
 
+def index_tables(slot_tile, rows, cap, bucket, group_tiles, row, half):
+    slots = slot_tile.shape[0]
+    width = HALF * cap
+    ids = jnp.arange(slots, dtype=jnp.int32)
+    block = lax.div(ids, width)
+    group = jnp.where(slot_tile >= 0, lax.div(slot_tile, group_tiles), rows)
+    key = block * (rows + 1) + group
+    rank = jnp.sum(
+        ((key[None, :] == key[:, None]) & (ids[None, :] < ids[:, None])).astype(jnp.int32), axis=1
+    )
+    arrival = (lax.rem(block, 2) * rows + lax.div(block, 2)) * bucket + rank
+    wanted = row * group_tiles + jnp.arange(group_tiles, dtype=jnp.int32)
+    pick = jnp.sum(jnp.where(slot_tile[None, :] == wanted[:, None], arrival[None, :], 0), axis=1)
+    inside = lax.rem(ids, width)
+    dev, pos = lax.div(inside, cap), lax.rem(inside, cap)
+    far_place = jnp.where(pos < BASE, dev * BASE + pos, HALF * BASE + pos - BASE)
+    places = jnp.arange(2 * rows * bucket, dtype=jnp.int32)
+    near = places < rows * bucket
+    want_block = row * 2 + jnp.where(near, half, 1 - half)
+    want = want_block * (slots * rows) + lax.rem(places, rows * bucket)
+    have = jnp.where(slot_tile >= 0, block * (slots * rows) + group * bucket + rank, -1)
+    value = jnp.where(block == row * 2 + half, inside, far_place)
+    send = jnp.sum(jnp.where(have[None, :] == want[:, None], value[None, :], 0), axis=1)
+    live = (block == row * 2 + half) & (pos == BASE) & (slot_tile >= 0)
+    full = jnp.sum(jnp.where(live, dev, 0))
+    return send, full[None], pick
+
+
+def encode(
+    rows, slabs, cap, bucket, group_tiles,
+    send_idx, full, pick_idx, pixels, w_space, b_space, w_time, b_time, gain,
+    out,
+    pix, ws, wt, plane, patch, spatial, lat,
+    near0, near1, far0, far1, relay0, relay1, relay_out, packed, rec0, rec1,
+    in_sem, w_sem, send_a, recv_n, recv_f, send_b, recv_r, send_r, send_y, recv_y,
+):
+    frames = 2
+    near, far, relay, rec = (near0, near1), (far0, far1), (relay0, relay1), (rec0, rec1)
+    f32, bf16 = jnp.float32, jnp.bfloat16
+    row = lax.axis_index("tile")
+    slab = lax.axis_index("tm")
+    half = lax.div(slab, HALF)
+    mine = lax.rem(slab, HALF)
+    first = (1 - half) * HALF
+    low = half * HALF
+    barrier = pltpu.get_barrier_semaphore()
+    for k in range(1, slabs):
+        pl.semaphore_signal(barrier, inc=1, device_id={"tm": lax.rem(slab + k, slabs)})
+    for k in range(1, rows):
+        pl.semaphore_signal(barrier, inc=1, device_id={"tile": lax.rem(row + k, rows)})
+
+    def load(s):
+        return pltpu.make_async_copy(
+            pixels.at[:, pl.ds(s * frames, frames)], pix.at[s], in_sem.at[s]
+        )
+
+    start = lax.rem(first + slabs - 1, slabs)
+    load(start).start()
+    ws_copy = pltpu.make_async_copy(w_space, ws, w_sem.at[0])
+    ws_copy.start()
+    load(first).start()
+    wt_copy = pltpu.make_async_copy(w_time, wt, w_sem.at[1])
+    wt_copy.start()
+
+    @pl.loop(1, slabs - 1)
+    def _(k):
+        load(lax.rem(first + k, slabs)).start()
+
+    count = frames * cap
+    side = TILE_SIDE
+    out_side = side // 2
+    area = out_side * out_side
+    height = count * area
+    channels = patch.shape[1] // 9
+    lanes = plane.shape[-1]
+    for piece in range(channels // lanes):
+        plane[1, piece, :, 8:16] = jnp.zeros((count, 8, lanes), f32)
+    spatial[pl.ds(0, height)] = jnp.zeros((height, spatial.shape[1]), bf16)
+    edge = lax.rem(lax.broadcasted_iota(jnp.int32, (area, lanes), 0), out_side) == 0
+
+    def conv(s):
+        load(s).wait()
+
+        @pl.loop(0, cap)
+        def _(p):
+            for f in range(frames):
+                image = f * cap + p
+                value = pix[s, p, f].astype(f32).reshape(out_side, 2, side, channels)
+                for parity in range(2):
+                    rows_of = value[:, parity].reshape(out_side * side, channels)
+                    for piece in range(channels // lanes):
+                        plane[parity, piece, image, 16:48] = rows_of[
+                            :, piece * lanes:(piece + 1) * lanes
+                        ]
+            for f in range(frames):
+                image = f * cap + p
+                for a in range(3):
+                    parity, base = ((1, 8), (0, 16), (1, 16))[a]
+                    for b in range(3):
+                        for piece in range(channels // lanes):
+                            taken = plane[
+                                parity, piece, image, pl.ds(base + b - 1, area, stride=2)
+                            ]
+                            if b == 0:
+                                taken = jnp.where(edge, 0.0, taken)
+                            at = (3 * a + b) * channels + piece * lanes
+                            patch[
+                                pl.ds(pl.multiple_of(image * area, area), area),
+                                at:at + lanes,
+                            ] = taken.astype(bf16)
+
+        total = jnp.dot(patch[...], ws[...], preferred_element_type=f32) + b_space[...]
+        active = total / (1.0 + jnp.exp(-total))
+        spatial[pl.ds(pl.multiple_of((s + 1) * height, height), height)] = active.astype(bf16)
+
+    def mix(s):
+        base = (s + 1) * height
+        step = height // frames
+        mixed = spatial[pl.ds(pl.multiple_of(base, step), height)].astype(f32) + b_time[...]
+        for lag in range(3):
+            mixed = mixed + jnp.dot(
+                spatial[pl.ds(pl.multiple_of(base - lag * step, step), height)],
+                wt[lag],
+                preferred_element_type=f32,
+            )
+        scale = lax.rsqrt(jnp.mean(mixed * mixed, axis=-1, keepdims=True) + 1e-06)
+        value = (mixed * scale * gain[...]).astype(bf16)
+        lat[s] = value.reshape(frames, cap, area, value.shape[-1])
+
+    def near_copy(f, j):
+        s = low + j
+        return pltpu.make_async_remote_copy(
+            src_ref=lat.at[s, f],
+            dst_ref=near[f].at[pl.ds(mine * cap, cap)],
+            send_sem=send_a.at[f, s],
+            recv_sem=recv_n.at[f, mine],
+            device_id={"tm": s},
+        )
+
+    def near_wait(f, j):
+        return pltpu.make_async_remote_copy(
+            src_ref=lat.at[low + j, f],
+            dst_ref=near[f].at[pl.ds(j * cap, cap)],
+            send_sem=send_a.at[f, low + j],
+            recv_sem=recv_n.at[f, j],
+            device_id={"tm": low + j},
+        )
+
+    def far_copy(f, j):
+        s = first + j
+        return pltpu.make_async_remote_copy(
+            src_ref=lat.at[s, f, pl.ds(0, BASE)],
+            dst_ref=far[f].at[pl.ds(mine * BASE, BASE)],
+            send_sem=send_a.at[f, s],
+            recv_sem=recv_f.at[f, mine],
+            device_id={"tm": s},
+        )
+
+    def far_wait(f, j):
+        return pltpu.make_async_remote_copy(
+            src_ref=lat.at[first + j, f, pl.ds(0, BASE)],
+            dst_ref=far[f].at[pl.ds(j * BASE, BASE)],
+            send_sem=send_a.at[f, first + j],
+            recv_sem=recv_f.at[f, j],
+            device_id={"tm": first + j},
+        )
+
+    def relay_copy(f, j):
+        return pltpu.make_async_remote_copy(
+            src_ref=lat.at[first + j, f, pl.ds(BASE, BASE)],
+            dst_ref=relay[f].at[pl.ds(mine * BASE, BASE)],
+            send_sem=send_b.at[f, j],
+            recv_sem=recv_r.at[f, mine],
+            device_id={"tm": low + j},
+        )
+
+    def relay_wait(f, j):
+        return pltpu.make_async_remote_copy(
+            src_ref=lat.at[first + j, f, pl.ds(BASE, BASE)],
+            dst_ref=relay[f].at[pl.ds(j * BASE, BASE)],
+            send_sem=send_b.at[f, j],
+            recv_sem=recv_r.at[f, j],
+            device_id={"tm": low + j},
+        )
+
+    def forward(f):
+        return pltpu.make_async_remote_copy(
+            src_ref=relay_out.at[f],
+            dst_ref=far[f].at[pl.ds(HALF * BASE, BASE)],
+            send_sem=send_r.at[f],
+            recv_sem=recv_f.at[f, HALF],
+            device_id={"tm": first + mine},
+        )
+
+    def tile_copy(c, f, k):
+        to = lax.rem(row + k, rows)
+        part = half if c == 0 else 1 - half
+        return pltpu.make_async_remote_copy(
+            src_ref=packed.at[c, f, pl.ds(to * bucket, bucket)],
+            dst_ref=rec[f].at[pl.ds((part * rows + row) * bucket, bucket)],
+            send_sem=send_y.at[c, f, k - 1],
+            recv_sem=recv_y.at[c, f, k - 1],
+            device_id={"tile": to},
+        )
+
+    def send_slab(f, k):
+        @pl.when(k < HALF)
+        def _():
+            j = k
+            far_copy(f, j).start()
+
+            @pl.when(j != mine)
+            def _():
+                relay_copy(f, j).start()
+
+            @pl.when(j == mine)
+            def _():
+                relay[f][pl.ds(mine * BASE, BASE)] = lat[first + mine, f, BASE:cap]
+
+        @pl.when(k >= HALF)
+        def _():
+            j = k - HALF
+
+            @pl.when(j != mine)
+            def _():
+                near_copy(f, j).start()
+
+            @pl.when(j == mine)
+            def _():
+                near[f][pl.ds(mine * cap, cap)] = lat[slab, f]
+
+    def run_relay(f):
+        for k in range(1, HALF):
+            relay_wait(f, lax.rem(mine + k, HALF)).wait_recv()
+        for i in range(BASE):
+            relay_out[f, i] = relay[f][full[0] * BASE + i]
+        forward(f).start()
+
+    def run_tiles(c, f):
+        if c == 0:
+            for k in range(1, HALF):
+                near_wait(f, lax.rem(mine + k, HALF)).wait_recv()
+        else:
+            for j in range(HALF):
+                far_wait(f, j).wait_recv()
+            forward(f).wait_recv()
+        source = near[f] if c == 0 else far[f]
+
+        @pl.loop(0, rows * bucket)
+        def _(i):
+            packed[c, f, i] = source[send_idx[c * rows * bucket + i]]
+
+        for k in range(1, rows):
+            tile_copy(c, f, k).start()
+        part = half if c == 0 else 1 - half
+        rec[f][pl.ds((part * rows + row) * bucket, bucket)] = packed[
+            c, f, pl.ds(row * bucket, bucket)
+        ]
+
+    ws_copy.wait()
+    conv(start)
+    pl.semaphore_wait(barrier, slabs + rows - 2)
+    wt_copy.wait()
+
+    @pl.loop(0, slabs)
+    def _(k):
+        s = lax.rem(first + k, slabs)
+
+        @pl.when(k < slabs - 1)
+        def _():
+            conv(s)
+
+        mix(s)
+        send_slab(0, k)
+
+    @pl.loop(0, slabs)
+    def _(k):
+        send_slab(1, k)
+
+    run_relay(0)
+    run_tiles(0, 0)
+    run_relay(1)
+    run_tiles(1, 0)
+    run_tiles(0, 1)
+    run_tiles(1, 1)
+
+    for f in range(frames):
+        for c in range(2):
+            for k in range(1, rows):
+                tile_copy(c, f, k).wait_recv()
+
+        @pl.loop(0, group_tiles)
+        def _(i):
+            out[i, f] = rec[f][pick_idx[i]]
+
+    for f in range(frames):
+        for k in range(1, HALF):
+            j = lax.rem(mine + k, HALF)
+            near_copy(f, j).wait_send()
+            relay_copy(f, j).wait_send()
+        for j in range(HALF):
+            far_copy(f, j).wait_send()
+        forward(f).wait_send()
+        for c in range(2):
+            for k in range(1, rows):
+                tile_copy(c, f, k).wait_send()
+
+
+def body_two_blocks(rows, slabs, pixels, slot_tile, w_space, b_space, w_time, b_time, gain):
+    cap, all_frames, pix_count, channels = pixels.shape
+    features = w_space.shape[-1]
+    frames = all_frames // slabs
+    group_tiles = cap // 2 * slabs
+    per_group = (cap + rows - 1) // rows
+    bucket = per_group * 3
+    row = lax.axis_index("tile")
+    half = lax.div(lax.axis_index("tm"), HALF)
+    send_idx, full, pick_idx = index_tables(
+        slot_tile, rows, cap, bucket, group_tiles, row, half
+    )
+    area = pix_count // 4
+    count = frames * cap
+    height = count * area
+    vmem = pl.BlockSpec(memory_space=pltpu.VMEM)
+    smem = pl.BlockSpec(memory_space=pltpu.SMEM)
+    hbm = pl.BlockSpec(memory_space=pl.ANY)
+    bf16, f32 = jnp.bfloat16, jnp.float32
+    dma = pltpu.SemaphoreType.DMA
+
+    def held(*lead):
+        return pltpu.VMEM(lead + (area, features), bf16)
+
+    return pl.pallas_call(
+        functools.partial(encode, rows, slabs, cap, bucket, group_tiles),
+        out_shape=jax.ShapeDtypeStruct((group_tiles, frames, area, features), bf16),
+        in_specs=[smem, smem, smem, hbm, hbm, vmem, hbm, vmem, vmem],
+        out_specs=vmem,
+        scratch_shapes=[
+            pltpu.VMEM((slabs, cap, frames, pix_count, channels), bf16),
+            pltpu.VMEM((9 * channels, features), bf16),
+            pltpu.VMEM((3, features, features), bf16),
+            pltpu.VMEM((2, channels // 128, count, 48, 128), f32),
+            pltpu.VMEM((height, 9 * channels), bf16),
+            pltpu.VMEM(((slabs + 1) * height, features), bf16),
+            held(slabs, frames, cap),
+            held(HALF * cap), held(HALF * cap),
+            held(HALF * BASE + BASE), held(HALF * BASE + BASE),
+            held(HALF * BASE), held(HALF * BASE),
+            held(frames, BASE),
+            held(2, frames, rows * bucket),
+            held(2 * rows * bucket), held(2 * rows * bucket),
+            dma((slabs,)), dma((2,)),
+            dma((frames, slabs)), dma((frames, HALF)), dma((frames, HALF + 1)),
+            dma((frames, HALF)), dma((frames, HALF)), dma((frames,)),
+            dma((2, frames, rows - 1)), dma((2, frames, rows - 1)),
+        ],
+        compiler_params=pltpu.CompilerParams(
+            collective_id=1, has_side_effects=True, vmem_limit_bytes=48 << 20
+        ),
+    )(
+        send_idx, full, pick_idx, pixels, w_space.reshape(9 * channels, features),
+        b_space[None], w_time, b_time[None], gain[None],
+    )
+
+
 def solution(mesh):
+    rows, slabs = mesh.shape["tile"], mesh.shape["tm"]
+    plan = body_two_blocks if slabs == 2 * HALF else body
     return jax.shard_map(
-        functools.partial(body, mesh.shape["tile"], mesh.shape["tm"]),
+        functools.partial(plan, rows, slabs),
         mesh=mesh,
         in_specs=(P(("tile", "tm"), None, None, None), P(), P(), P(), P(), P(), P()),
         out_specs=P("tile", "tm", None, None),

time: 77.3 us -> 57.4 us (0.74)
  the two profiles are of different devices: /device:TPU:21 before, /device:TPU:17 now
where the time goes in v1:
time: 57.4 us; the launch traced here: 57.1 us
  Pallas kernels  47.8 us (83%)
  local copies, waits for them, and re-layouts  6 us (10%)
  other arithmetic  3.25 us (6%)
    pallas_call x1, Pallas kernels, body_two_blocks(): pl.pallas_call(functools.partial(encode, rows, slabs, cap, bucket, group_...  47.8 us
    unnamed x11, local copies, waits for them, and re-layouts  6 us
    add x1, other arithmetic, index_tables(): arrival = (lax.rem(block, 2) * rows + lax.div(block, 2)) * bucket + rank  1.34 us

profile of v1, /device:TPU:17, one launch (start us, length us, event | category | flops | bytes accessed | tf_op | source)
XLA Modules:
  0.0 57.1 jit_solution(17435340783665717493)
XLA Ops:
  0.0 0.7 %multiply_add_fusion = s32[192]{0:T(256)S(1)} fusion(s32[192]{0:T(256)} %param.8), kind=kLoop, calls=%fused_computation.21 | loop fusion | flops 1152 | bytes 1536 | tf_op jit(solution)/shard_map/add | solution.py:233
  0.7 0.2 convert_reduce_fusion
  0.9 1.3 %fusion.4 = (s32[192]{0:T(256)S(1)}, s32[192]{0:T(256)S(1)}, s32[]{:T(128)}, s32[192]{0:T(256)S(1)}) fusion(s32[192]{0:T(256)S(1)} %convert_reduce_fusion, s32[192]{0:T(256)} %param.8, s32[]{:T(128)S(6)} %add.77), kind=kLoop, calls=%fused_computation.15 | loop fusion | flops 7103 | bytes 3848 | tf_op jit(solution)/shard_map/add | solution.py:237
  2.2 0.9 %select_reduce_fusion.1.pick_idx = s32[24]{0:T(128)S(1)} fusion(s32[192]{0:T(256)S(1)} %get-tuple-element.5, s32[192]{0:T(256)} %param.8, s32[24]{0:T(128)S(1)} %iota_add_fusion), kind=kLoop, calls=%fused_computation.4 | loop fusion | flops 13800 | bytes 1728 | tf_op jit(solution)/shard_map/reduce_sum | solution.py:239
  3.1 0.2 select_reduce_fusion.send_idx
  3.3 0.0 copy-start
  3.3 1.7 %copy-done = bf16[3,3,256,512]{3,2,1,0:T(8,128)(2,1)S(1)} copy-done((bf16[3,3,256,512]{3,2,1,0:T(8,128)(2,1)S(1)}, bf16[3,3,256,512]{3,2,1,0:T(8,128)(2,1)}, u32[]{:S(2)}) %copy-start) | copy-done | bytes 2359320
  4.9 0.0 copy-start.1
  5.0 1.4 %copy-done.1 = bf16[3,512,512]{2,1,0:T(8,128)(2,1)S(1)} copy-done((bf16[3,512,512]{2,1,0:T(8,128)(2,1)S(1)}, bf16[3,512,512]{2,1,0:T(8,128)(2,1)}, u32[]{:S(2)}) %copy-start.1) | copy-done | bytes 1572888
  6.4 0.0 copy-start.2
  6.4 0.7 %copy-done.2 = f32[512]{0:T(512)S(1)} copy-done((f32[512]{0:T(512)S(1)}, f32[512]{0:T(512)}, u32[]{:S(2)}) %copy-start.2) | copy-done | bytes 2072
  7.0 0.0 copy-start.3
  7.0 0.7 %copy-done.3 = f32[512]{0:T(512)S(1)} copy-done((f32[512]{0:T(512)S(1)}, f32[512]{0:T(512)}, u32[]{:S(2)}) %copy-start.3) | copy-done | bytes 2072
  7.7 0.0 copy-start.4
  7.7 0.7 %copy-done.4 = f32[512]{0:T(512)S(1)} copy-done((f32[512]{0:T(512)S(1)}, f32[512]{0:T(512)}, u32[]{:S(2)}) %copy-start.4) | copy-done | bytes 2072
  8.4 47.8 %shard_map.73 = bf16[24,2,16,512]{3,2,1,0:T(8,128)(2,1)S(1)} custom-call(s32[48]{0:T(128)S(1)} %select_reduce_fusion.send_idx, s32[1]{0:T(128)} %bitcast.full, s32[24]{0:T(128)S(1)} %select_reduce_fusion.1.pick_idx, bf16[6,16,64,256]{3,2,1,0:T(8,128)(2,1)} %pixels.1, bf16[2304,512]{1,0:T(8,128)(2,1)S(1)} %bitcast.5, f32[1,512]{1,0:T(1,128)S(1)} %bitcast.6, ...), custom_call_target="tpu_custom_call" | custom-call | tf_op jit(solution)/shard_map/pallas_call | solution.py:559
  56.3 0.9 %copy.9 = bf16[24,2,16,512]{3,2,1,0:T(8,128)(2,1)} copy(bf16[24,2,16,512]{3,2,1,0:T(8,128)(2,1)S(1)} %shard_map.73) | data formatting | bytes 1572864
  (2 shorter events, 0.0 us)
Async XLA Ops:
  3.3 1.7 %copy-start = (bf16[3,3,256,512]{3,2,1,0:T(8,128)(2,1)S(1)}, bf16[3,3,256,512]{3,2,1,0:T(8,128)(2,1)}, u32[]{:S(2)}) copy-start(bf16[3,3,256,512]{3,2,1,0:T(8,128)(2,1)} %param.9) | copy-start | bytes 7077892
  4.9 1.4 %copy-start.1 = (bf16[3,512,512]{2,1,0:T(8,128)(2,1)S(1)}, bf16[3,512,512]{2,1,0:T(8,128)(2,1)}, u32[]{:S(2)}) copy-start(bf16[3,512,512]{2,1,0:T(8,128)(2,1)} %w_time.1) | copy-start | bytes 4718596
  6.4 0.7 %copy-start.2 = (f32[512]{0:T(512)S(1)}, f32[512]{0:T(512)}, u32[]{:S(2)}) copy-start(f32[512]{0:T(512)} %param.10) | copy-start | bytes 6148
  7.0 0.7 %copy-start.3 = (f32[512]{0:T(512)S(1)}, f32[512]{0:T(512)}, u32[]{:S(2)}) copy-start(f32[512]{0:T(512)} %param.12) | copy-start | bytes 6148
  7.7 0.7 %copy-start.4 = (f32[512]{0:T(512)S(1)}, f32[512]{0:T(512)}, u32[]{:S(2)}) copy-start(f32[512]{0:T(512)} %param.13) | copy-start | bytes 6148

commit v2 on v1

--- a/solution.py
+++ b/solution.py
@@ -224,39 +224,73 @@
     )(send_idx, pick_idx, spatial, w_time, b_time[None], gain[None])
 
 
-def index_tables(slot_tile, rows, cap, bucket, group_tiles, row, half):
-    slots = slot_tile.shape[0]
+def index_row(tiles, rows, cap, bucket, group_tiles, row, half):
+    slots = tiles.shape[1]
     width = HALF * cap
-    ids = jnp.arange(slots, dtype=jnp.int32)
-    block = lax.div(ids, width)
-    group = jnp.where(slot_tile >= 0, lax.div(slot_tile, group_tiles), rows)
-    key = block * (rows + 1) + group
-    rank = jnp.sum(
-        ((key[None, :] == key[:, None]) & (ids[None, :] < ids[:, None])).astype(jnp.int32), axis=1
-    )
-    arrival = (lax.rem(block, 2) * rows + lax.div(block, 2)) * bucket + rank
-    wanted = row * group_tiles + jnp.arange(group_tiles, dtype=jnp.int32)
-    pick = jnp.sum(jnp.where(slot_tile[None, :] == wanted[:, None], arrival[None, :], 0), axis=1)
-    inside = lax.rem(ids, width)
-    dev, pos = lax.div(inside, cap), lax.rem(inside, cap)
+    shape = (slots, slots)
+    along = lax.broadcasted_iota(jnp.int32, shape, 1)
+    down = lax.broadcasted_iota(jnp.int32, shape, 0)
+    spread = jnp.broadcast_to(tiles, shape)
+    column = jnp.sum(jnp.where(along == down, spread, 0), axis=1, keepdims=True)
+
+    def key_of(ids, tile):
+        key = jnp.where(tile < 0, rows, 0)
+        for k in range(1, rows):
+            key = key + jnp.where(tile >= k * group_tiles, 1, 0)
+        block = jnp.zeros_like(ids)
+        for k in range(1, slots // width):
+            block = block + jnp.where(ids >= k * width, 1, 0)
+        return block, key
+
+    ids = lax.broadcasted_iota(jnp.int32, (slots, 1), 0)
+    block, group = key_of(ids, column)
+    lane = lax.broadcasted_iota(jnp.int32, (1, slots), 1)
+    block_r, group_r = key_of(lane, tiles)
+    same = (block * (rows + 1) + group) == (block_r * (rows + 1) + group_r)
+    rank = jnp.sum(jnp.where(same & (along < down), 1, 0), axis=1, keepdims=True)
+    part = block % 2
+    arrival = (part * rows + block // 2) * bucket + rank
+    inside = ids - block * width
+    dev = jnp.zeros_like(ids)
+    for k in range(1, HALF):
+        dev = dev + jnp.where(inside >= k * cap, 1, 0)
+    pos = inside - dev * cap
     far_place = jnp.where(pos < BASE, dev * BASE + pos, HALF * BASE + pos - BASE)
-    places = jnp.arange(2 * rows * bucket, dtype=jnp.int32)
-    near = places < rows * bucket
-    want_block = row * 2 + jnp.where(near, half, 1 - half)
-    want = want_block * (slots * rows) + lax.rem(places, rows * bucket)
-    have = jnp.where(slot_tile >= 0, block * (slots * rows) + group * bucket + rank, -1)
-    value = jnp.where(block == row * 2 + half, inside, far_place)
-    send = jnp.sum(jnp.where(have[None, :] == want[:, None], value[None, :], 0), axis=1)
-    live = (block == row * 2 + half) & (pos == BASE) & (slot_tile >= 0)
-    full = jnp.sum(jnp.where(live, dev, 0))
-    return send, full[None], pick
+    mine = block == row * 2 + half
+    other = block == row * 2 + 1 - half
+    live = column >= 0
+    value = jnp.where(mine, inside, far_place)
+    places = rows * bucket
+    target = jnp.where(
+        live & (mine | other), group * bucket + rank + jnp.where(other, places, 0), -1
+    )
+    place = lax.broadcasted_iota(jnp.int32, (1, 128), 1)
+    wanted = jnp.where(
+        (place >= 2 * places) & (place < 2 * places + group_tiles),
+        place - 2 * places + row * group_tiles,
+        -2,
+    )
+    total = jnp.where(target == place, value, 0) + jnp.where(column == wanted, arrival, 0)
+    total = total + jnp.where(
+        (mine & live & (pos == BASE)) & (place == 2 * places + group_tiles), dev, 0
+    )
+    limit = jnp.where(
+        place < places,
+        width,
+        jnp.where(
+            place < 2 * places,
+            (HALF + 1) * BASE,
+            jnp.where(place < 2 * places + group_tiles, 2 * places, HALF),
+        ),
+    )
+    return jnp.minimum(jnp.sum(total, axis=0, keepdims=True), limit - 1)
 
 
 def encode(
     rows, slabs, cap, bucket, group_tiles,
-    send_idx, full, pick_idx, pixels, w_space, b_space, w_time, b_time, gain,
+    slot_tile, pixels, w_space, b_space_h, w_time, b_time_h, gain_h,
     out,
-    pix, ws, wt, plane, patch, spatial, lat,
+    pix, ws, wt, b_space, b_time, gain, tiles, index_v, index, plane, patch, spatial, lat,
     near0, near1, far0, far1, relay0, relay1, relay_out, packed, rec0, rec1,
     in_sem, w_sem, send_a, recv_n, recv_f, send_b, recv_r, send_r, send_y, recv_y,
 ):
@@ -282,6 +316,14 @@
 
     start = lax.rem(first + slabs - 1, slabs)
     load(start).start()
+    small = [
+        pltpu.make_async_copy(source, target, w_sem.at[2 + i])
+        for i, (source, target) in enumerate(
+            ((b_space_h, b_space), (b_time_h, b_time), (gain_h, gain), (slot_tile, tiles))
+        )
+    ]
+    for copy in small:
+        copy.start()
     ws_copy = pltpu.make_async_copy(w_space, ws, w_sem.at[0])
     ws_copy.start()
     load(first).start()
@@ -459,7 +501,7 @@
         for k in range(1, HALF):
             relay_wait(f, lax.rem(mine + k, HALF)).wait_recv()
         for i in range(BASE):
-            relay_out[f, i] = relay[f][full[0] * BASE + i]
+            relay_out[f, i] = relay[f][index[0, full_at] * BASE + i]
         forward(f).start()
 
     def run_tiles(c, f):
@@ -474,7 +516,7 @@
 
         @pl.loop(0, rows * bucket)
         def _(i):
-            packed[c, f, i] = source[send_idx[c * rows * bucket + i]]
+            packed[c, f, i] = source[index[0, c * rows * bucket + i]]
 
         for k in range(1, rows):
             tile_copy(c, f, k).start()
@@ -483,6 +525,8 @@
             c, f, pl.ds(row * bucket, bucket)
         ]
 
+    for copy in small:
+        copy.wait()
     ws_copy.wait()
     conv(start)
     pl.semaphore_wait(barrier, slabs + rows - 2)
@@ -499,15 +543,26 @@
         mix(s)
         send_slab(0, k)
 
-    @pl.loop(0, slabs)
+        @pl.when(k >= HALF)
+        def _():
+            send_slab(1, k)
+
+    @pl.loop(0, HALF)
     def _(k):
         send_slab(1, k)
 
+    index_v[...] = index_row(tiles[...], rows, cap, bucket, group_tiles, row, half)
+    index_copy = pltpu.make_async_copy(index_v, index, w_sem.at[6])
+    index_copy.start()
+    index_copy.wait()
+    pick_at = 2 * rows * bucket
+    full_at = pick_at + group_tiles
+
     run_relay(0)
     run_tiles(0, 0)
-    run_relay(1)
     run_tiles(1, 0)
     run_tiles(0, 1)
+    run_relay(1)
     run_tiles(1, 1)
 
     for f in range(frames):
@@ -517,7 +572,7 @@
 
         @pl.loop(0, group_tiles)
         def _(i):
-            out[i, f] = rec[f][pick_idx[i]]
+            out[i, f] = rec[f][index[0, pick_at + i]]
 
     for f in range(frames):
         for k in range(1, HALF):
@@ -539,16 +594,10 @@
     group_tiles = cap // 2 * slabs
     per_group = (cap + rows - 1) // rows
     bucket = per_group * 3
-    row = lax.axis_index("tile")
-    half = lax.div(lax.axis_index("tm"), HALF)
-    send_idx, full, pick_idx = index_tables(
-        slot_tile, rows, cap, bucket, group_tiles, row, half
-    )
     area = pix_count // 4
     count = frames * cap
     height = count * area
     vmem = pl.BlockSpec(memory_space=pltpu.VMEM)
-    smem = pl.BlockSpec(memory_space=pltpu.SMEM)
     hbm = pl.BlockSpec(memory_space=pl.ANY)
     bf16, f32 = jnp.bfloat16, jnp.float32
     dma = pltpu.SemaphoreType.DMA
@@ -559,12 +608,18 @@
     return pl.pallas_call(
         functools.partial(encode, rows, slabs, cap, bucket, group_tiles),
         out_shape=jax.ShapeDtypeStruct((group_tiles, frames, area, features), bf16),
-        in_specs=[smem, smem, smem, hbm, hbm, vmem, hbm, vmem, vmem],
+        in_specs=[hbm] * 7,
         out_specs=vmem,
         scratch_shapes=[
             pltpu.VMEM((slabs, cap, frames, pix_count, channels), bf16),
             pltpu.VMEM((9 * channels, features), bf16),
             pltpu.VMEM((3, features, features), bf16),
+            pltpu.VMEM((1, features), f32),
+            pltpu.VMEM((1, features), f32),
+            pltpu.VMEM((1, features), f32),
+            pltpu.VMEM((1, slot_tile.shape[0]), jnp.int32),
+            pltpu.VMEM((1, 128), jnp.int32),
+            pltpu.SMEM((1, 128), jnp.int32),
             pltpu.VMEM((2, channels // 128, count, 48, 128), f32),
             pltpu.VMEM((height, 9 * channels), bf16),
             pltpu.VMEM(((slabs + 1) * height, features), bf16),
@@ -575,16 +630,16 @@
             held(frames, BASE),
             held(2, frames, rows * bucket),
             held(2 * rows * bucket), held(2 * rows * bucket),
-            dma((slabs,)), dma((2,)),
+            dma((slabs,)), dma((7,)),
             dma((frames, slabs)), dma((frames, HALF)), dma((frames, HALF + 1)),
             dma((frames, HALF)), dma((frames, HALF)), dma((frames,)),
             dma((2, frames, rows - 1)), dma((2, frames, rows - 1)),
         ],
         compiler_params=pltpu.CompilerParams(
-            collective_id=1, has_side_effects=True, vmem_limit_bytes=48 << 20
+            collective_id=1, has_side_effects=True, vmem_limit_bytes=62 << 20
         ),
     )(
-        send_idx, full, pick_idx, pixels, w_space.reshape(9 * channels, features),
+        slot_tile[None], pixels, w_space.reshape(9 * channels, features),
         b_space[None], w_time, b_time[None], gain[None],
     )
 

time: 57.4 us -> 49.7 us (0.87)
  local copies, waits for them, and re-layouts: 6 us -> 2.09 us
  other arithmetic: 3.25 us -> 0 us
    unnamed x11 -> x1, local copies, waits for them, and re-layouts: 6 us -> 2.09 us
    add x4 -> x0, other arithmetic: 2.04 us -> none  [the longest x1 1.34 us: index_tables(): arrival = (lax.rem(block, 2) * rows + lax.div(block, 2)) * bucket + rank]
    reduce_sum x3 -> x0, other arithmetic: 1.22 us -> none  [the longest x1 0.86 us: index_tables(): jnp.sum(jnp.where(slot_tile[None, :] == wanted[:, None], arrival[None, :]...]
where the time goes in v2:
time: 49.7 us; the launch traced here: 49.6 us
  Pallas kernels  47.5 us (96%)
  local copies, waits for them, and re-layouts  2.09 us (4%)
    pallas_call x1, Pallas kernels, body_two_blocks(): pl.pallas_call(functools.partial(encode, rows, slabs, cap, bucket, group_...  47.5 us
    unnamed x1, local copies, waits for them, and re-layouts  2.09 us

profile of v2, /device:TPU:17, one launch (start us, length us, event | category | flops | bytes accessed | tf_op | source)
XLA Modules:
  0.0 49.6 jit_solution(1893190802093891666)
XLA Ops:
  0.0 47.5 %shard_map.73 = bf16[24,2,16,512]{3,2,1,0:T(8,128)(2,1)} custom-call(s32[1,192]{1,0:T(1,128)} %bitcast.9, bf16[6,16,64,256]{3,2,1,0:T(8,128)(2,1)} %pixels.1, bf16[2304,512]{1,0:T(8,128)(2,1)} %bitcast.5, f32[1,512]{1,0:T(1,128)} %bitcast.6, bf16[3,512,512]{2,1,0:T(8,128)(2,1)} %w_time.1, f32[1,512]{1,0:T(1,128)} %bitcast.7, f32[1,512]{1,0:T(1,128)} %bitcast.8), custom_call_target="tpu_custom_call" | custom-call | tf_op jit(solution)/shard_map/pallas_call | solution.py:608
  47.5 2.1 %copy.9 = bf16[24,2,16,512]{3,2,1,0:T(8,128)(2,1)} copy(bf16[24,2,16,512]{3,2,1,0:T(8,128)(2,1)} %shard_map.73) | data formatting | bytes 1572864

commit v3 on v2

--- a/solution.py
+++ b/solution.py
@@ -255,11 +255,10 @@
     for k in range(1, HALF):
         dev = dev + jnp.where(inside >= k * cap, 1, 0)
     pos = inside - dev * cap
-    far_place = jnp.where(pos < BASE, dev * BASE + pos, HALF * BASE + pos - BASE)
+    came = jnp.where(pos < BASE, dev * BASE + pos, HALF * BASE + pos - BASE)
     mine = block == row * 2 + half
     other = block == row * 2 + 1 - half
     live = column >= 0
-    value = jnp.where(mine, inside, far_place)
     places = rows * bucket
     target = jnp.where(
         live & (mine | other), group * bucket + rank + jnp.where(other, places, 0), -1
@@ -270,18 +269,14 @@
         place - 2 * places + row * group_tiles,
         -2,
     )
-    total = jnp.where(target == place, value, 0) + jnp.where(column == wanted, arrival, 0)
-    total = total + jnp.where(
-        (mine & live & (pos == BASE)) & (place == 2 * places + group_tiles), dev, 0
-    )
+    total = jnp.where(target == place, came, 0) + jnp.where(column == wanted, arrival, 0)
+    full = mine & live & (pos == BASE)
+    for at, part_of in ((0, dev // 2), (1, dev % 2)):
+        total = total + jnp.where(full & (place == 2 * places + group_tiles + at), part_of, 0)
     limit = jnp.where(
-        place < places,
-        width,
-        jnp.where(
-            place < 2 * places,
-            (HALF + 1) * BASE,
-            jnp.where(place < 2 * places + group_tiles, 2 * places, HALF),
-        ),
+        place < 2 * places,
+        (HALF + 1) * BASE,
+        jnp.where(place < 2 * places + group_tiles, 2 * places, 2),
     )
     return jnp.minimum(jnp.sum(total, axis=0, keepdims=True), limit - 1)
 
@@ -291,76 +286,87 @@
     slot_tile, pixels, w_space, b_space_h, w_time, b_time_h, gain_h,
     out,
     pix, ws, wt, b_space, b_time, gain, tiles, index_v, index, plane, patch, spatial, lat,
-    near0, near1, far0, far1, relay0, relay1, relay_out, packed, rec0, rec1,
-    in_sem, w_sem, send_a, recv_n, recv_f, send_b, recv_r, send_r, send_y, recv_y,
+    near, far0, far1, x_near, x_far, z_near, z_far, z_out, forward_out,
+    packed_n, packed_f, rec,
+    in_sem, w_sem, send_n, recv_n, send_f, recv_f, send_x, recv_x, send_z, recv_z,
+    send_r, send_yn, recv_yn, send_yf, recv_yf,
 ):
     frames = 2
-    near, far, relay, rec = (near0, near1), (far0, far1), (relay0, relay1), (rec0, rec1)
+    far = (far0, far1)
     f32, bf16 = jnp.float32, jnp.bfloat16
     row = lax.axis_index("tile")
     slab = lax.axis_index("tm")
     half = lax.div(slab, HALF)
     mine = lax.rem(slab, HALF)
+    x = lax.rem(slab, 2)
+    zl = lax.div(mine, 2)
     first = (1 - half) * HALF
     low = half * HALF
+    x_peer = slab + 1 - 2 * x
+    z_peer = slab + 2 - 4 * zl
     barrier = pltpu.get_barrier_semaphore()
     for k in range(1, slabs):
         pl.semaphore_signal(barrier, inc=1, device_id={"tm": lax.rem(slab + k, slabs)})
     for k in range(1, rows):
         pl.semaphore_signal(barrier, inc=1, device_id={"tile": lax.rem(row + k, rows)})
 
-    def load(s):
+    steps = slabs // 2
+    span = 2 * frames
+    origin = lax.div(first, 2)
+
+    def load(z):
         return pltpu.make_async_copy(
-            pixels.at[:, pl.ds(s * frames, frames)], pix.at[s], in_sem.at[s]
-        )
-
-    start = lax.rem(first + slabs - 1, slabs)
-    load(start).start()
+            pixels.at[:, pl.ds(z * span, span)], pix.at[z], in_sem.at[z]
+        )
+
+    start = lax.rem(origin + steps - 1, steps)
     small = [
         pltpu.make_async_copy(source, target, w_sem.at[2 + i])
         for i, (source, target) in enumerate(
-            ((b_space_h, b_space), (b_time_h, b_time), (gain_h, gain), (slot_tile, tiles))
+            ((slot_tile, tiles), (b_space_h, b_space), (b_time_h, b_time), (gain_h, gain))
         )
     ]
     for copy in small:
         copy.start()
+    load(start).start()
     ws_copy = pltpu.make_async_copy(w_space, ws, w_sem.at[0])
     ws_copy.start()
-    load(first).start()
+    load(origin).start()
     wt_copy = pltpu.make_async_copy(w_time, wt, w_sem.at[1])
     wt_copy.start()
 
-    @pl.loop(1, slabs - 1)
+    @pl.loop(1, steps - 1)
     def _(k):
-        load(lax.rem(first + k, slabs)).start()
-
-    count = frames * cap
+        load(lax.rem(origin + k, steps)).start()
+
+    count = span * cap
     side = TILE_SIDE
     out_side = side // 2
     area = out_side * out_side
     height = count * area
+    step_rows = height // span
     channels = patch.shape[1] // 9
     lanes = plane.shape[-1]
     for piece in range(channels // lanes):
         plane[1, piece, :, 8:16] = jnp.zeros((count, 8, lanes), f32)
-    spatial[pl.ds(0, height)] = jnp.zeros((height, spatial.shape[1]), bf16)
+    spatial[height - 2 * step_rows:height] = jnp.zeros((2 * step_rows, spatial.shape[1]), bf16)
     edge = lax.rem(lax.broadcasted_iota(jnp.int32, (area, lanes), 0), out_side) == 0
 
-    def conv(s):
-        load(s).wait()
+    def conv(z):
+        load(z).wait()
 
         @pl.loop(0, cap)
         def _(p):
-            for f in range(frames):
+            for f in range(span):
                 image = f * cap + p
-                value = pix[s, p, f].astype(f32).reshape(out_side, 2, side, channels)
+                value = pix[z, p, f].astype(f32).reshape(out_side, 2, side, channels)
                 for parity in range(2):
                     rows_of = value[:, parity].reshape(out_side * side, channels)
                     for piece in range(channels // lanes):
                         plane[parity, piece, image, 16:48] = rows_of[
                             :, piece * lanes:(piece + 1) * lanes
                         ]
-            for f in range(frames):
+            for f in range(span):
                 image = f * cap + p
                 for a in range(3):
                     parity, base = ((1, 8), (0, 16), (1, 16))[a]
@@ -379,212 +385,222 @@
 
         total = jnp.dot(patch[...], ws[...], preferred_element_type=f32) + b_space[...]
         active = total / (1.0 + jnp.exp(-total))
-        spatial[pl.ds(pl.multiple_of((s + 1) * height, height), height)] = active.astype(bf16)
-
-    def mix(s):
-        base = (s + 1) * height
-        step = height // frames
-        mixed = spatial[pl.ds(pl.multiple_of(base, step), height)].astype(f32) + b_time[...]
+        spatial[pl.ds(pl.multiple_of((z + 1) * height, height), height)] = active.astype(bf16)
+
+    def mix(z):
+        base = (z + 1) * height
+        mixed = spatial[pl.ds(pl.multiple_of(base, step_rows), height)].astype(f32) + b_time[...]
         for lag in range(3):
             mixed = mixed + jnp.dot(
-                spatial[pl.ds(pl.multiple_of(base - lag * step, step), height)],
+                spatial[pl.ds(pl.multiple_of(base - lag * step_rows, step_rows), height)],
                 wt[lag],
                 preferred_element_type=f32,
             )
         scale = lax.rsqrt(jnp.mean(mixed * mixed, axis=-1, keepdims=True) + 1e-06)
         value = (mixed * scale * gain[...]).astype(bf16)
-        lat[s] = value.reshape(frames, cap, area, value.shape[-1])
-
-    def near_copy(f, j):
-        s = low + j
-        return pltpu.make_async_remote_copy(
-            src_ref=lat.at[s, f],
-            dst_ref=near[f].at[pl.ds(mine * cap, cap)],
-            send_sem=send_a.at[f, s],
-            recv_sem=recv_n.at[f, mine],
-            device_id={"tm": s},
-        )
-
-    def near_wait(f, j):
-        return pltpu.make_async_remote_copy(
-            src_ref=lat.at[low + j, f],
-            dst_ref=near[f].at[pl.ds(j * cap, cap)],
-            send_sem=send_a.at[f, low + j],
-            recv_sem=recv_n.at[f, j],
+        lat[pl.ds(2 * z, 2)] = value.reshape(2, frames, cap, area, value.shape[-1])
+
+
+    def near_copy(j, source):
+        return pltpu.make_async_remote_copy(
+            src_ref=lat.at[low + j, :, pl.ds(0, BASE)],
+            dst_ref=near.at[:, pl.ds(source * BASE, BASE)],
+            send_sem=send_n.at[j],
+            recv_sem=recv_n.at[source],
             device_id={"tm": low + j},
         )
 
-    def far_copy(f, j):
-        s = first + j
-        return pltpu.make_async_remote_copy(
-            src_ref=lat.at[s, f, pl.ds(0, BASE)],
-            dst_ref=far[f].at[pl.ds(mine * BASE, BASE)],
-            send_sem=send_a.at[f, s],
-            recv_sem=recv_f.at[f, mine],
-            device_id={"tm": s},
-        )
-
-    def far_wait(f, j):
+    def far_copy(f, j, source):
         return pltpu.make_async_remote_copy(
             src_ref=lat.at[first + j, f, pl.ds(0, BASE)],
-            dst_ref=far[f].at[pl.ds(j * BASE, BASE)],
-            send_sem=send_a.at[f, first + j],
-            recv_sem=recv_f.at[f, j],
+            dst_ref=far[f].at[pl.ds(source * BASE, BASE)],
+            send_sem=send_f.at[f, j],
+            recv_sem=recv_f.at[f, source],
             device_id={"tm": first + j},
         )
 
-    def relay_copy(f, j):
-        return pltpu.make_async_remote_copy(
-            src_ref=lat.at[first + j, f, pl.ds(BASE, BASE)],
-            dst_ref=relay[f].at[pl.ds(mine * BASE, BASE)],
-            send_sem=send_b.at[f, j],
-            recv_sem=recv_r.at[f, mine],
-            device_id={"tm": low + j},
-        )
-
-    def relay_wait(f, j):
-        return pltpu.make_async_remote_copy(
-            src_ref=lat.at[first + j, f, pl.ds(BASE, BASE)],
-            dst_ref=relay[f].at[pl.ds(j * BASE, BASE)],
-            send_sem=send_b.at[f, j],
-            recv_sem=recv_r.at[f, j],
-            device_id={"tm": low + j},
+
+    def x_copy(c, place):
+        s = (low if c == 0 else first) + 2 * place + 1 - x
+        return pltpu.make_async_remote_copy(
+            src_ref=lat.at[s, :, pl.ds(BASE, BASE)],
+            dst_ref=(x_near if c == 0 else x_far).at[place, x],
+            send_sem=send_x.at[c, place],
+            recv_sem=recv_x.at[c, place],
+            device_id={"tm": x_peer},
+        )
+
+    def z_copy(c):
+        return pltpu.make_async_remote_copy(
+            src_ref=z_out.at[c],
+            dst_ref=(z_near if c == 0 else z_far).at[zl],
+            send_sem=send_z.at[c],
+            recv_sem=recv_z.at[c],
+            device_id={"tm": z_peer},
         )
 
     def forward(f):
         return pltpu.make_async_remote_copy(
-            src_ref=relay_out.at[f],
+            src_ref=forward_out.at[f],
             dst_ref=far[f].at[pl.ds(HALF * BASE, BASE)],
             send_sem=send_r.at[f],
             recv_sem=recv_f.at[f, HALF],
             device_id={"tm": first + mine},
         )
 
-    def tile_copy(c, f, k):
+    pick_at = 2 * rows * bucket
+    full_at = pick_at + group_tiles
+
+    def merge_x(c):
+        source, target, base = (x_near, z_near, low) if c == 0 else (x_far, z_far, first)
+        for place in range(2):
+            x_copy(c, place).wait_recv()
+            source[place, x] = lat[base + 2 * place + x, :, BASE:cap]
+        full_x = index[0, full_at + 1]
+        z_out[c] = source[1 - zl, full_x]
+        target[zl] = source[zl, full_x]
+        z_copy(c).start()
+
+    def merge_z_far():
+        z_copy(1).wait_recv()
+        forward_out[...] = z_far[index[0, full_at]]
+        for f in range(frames):
+            forward(f).start()
+
+    def merge_z_near():
+        z_copy(0).wait_recv()
+        near[:, HALF * BASE:] = z_near[index[0, full_at]]
+
+
+    def tile_near(k):
         to = lax.rem(row + k, rows)
-        part = half if c == 0 else 1 - half
-        return pltpu.make_async_remote_copy(
-            src_ref=packed.at[c, f, pl.ds(to * bucket, bucket)],
-            dst_ref=rec[f].at[pl.ds((part * rows + row) * bucket, bucket)],
-            send_sem=send_y.at[c, f, k - 1],
-            recv_sem=recv_y.at[c, f, k - 1],
+        return pltpu.make_async_remote_copy(
+            src_ref=packed_n.at[:, pl.ds(to * bucket, bucket)],
+            dst_ref=rec.at[:, pl.ds((half * rows + row) * bucket, bucket)],
+            send_sem=send_yn.at[k - 1],
+            recv_sem=recv_yn.at[k - 1],
             device_id={"tile": to},
         )
 
-    def send_slab(f, k):
-        @pl.when(k < HALF)
-        def _():
-            j = k
-            far_copy(f, j).start()
-
-            @pl.when(j != mine)
-            def _():
-                relay_copy(f, j).start()
-
-            @pl.when(j == mine)
-            def _():
-                relay[f][pl.ds(mine * BASE, BASE)] = lat[first + mine, f, BASE:cap]
-
-        @pl.when(k >= HALF)
-        def _():
-            j = k - HALF
-
-            @pl.when(j != mine)
-            def _():
-                near_copy(f, j).start()
-
-            @pl.when(j == mine)
-            def _():
-                near[f][pl.ds(mine * cap, cap)] = lat[slab, f]
-
-    def run_relay(f):
+    def tile_far(f, k):
+        to = lax.rem(row + k, rows)
+        return pltpu.make_async_remote_copy(
+            src_ref=packed_f.at[f, pl.ds(to * bucket, bucket)],
+            dst_ref=rec.at[f, pl.ds(((1 - half) * rows + row) * bucket, bucket)],
+            send_sem=send_yf.at[f, k - 1],
+            recv_sem=recv_yf.at[f, k - 1],
+            device_id={"tile": to},
+        )
+
+    def run_near():
         for k in range(1, HALF):
-            relay_wait(f, lax.rem(mine + k, HALF)).wait_recv()
-        for i in range(BASE):
-            relay_out[f, i] = relay[f][index[0, full_at] * BASE + i]
-        forward(f).start()
-
-    def run_tiles(c, f):
-        if c == 0:
-            for k in range(1, HALF):
-                near_wait(f, lax.rem(mine + k, HALF)).wait_recv()
-        else:
-            for j in range(HALF):
-                far_wait(f, j).wait_recv()
-            forward(f).wait_recv()
-        source = near[f] if c == 0 else far[f]
+            near_copy(mine, lax.rem(mine + k, HALF)).wait_recv()
+        merge_z_near()
 
         @pl.loop(0, rows * bucket)
         def _(i):
-            packed[c, f, i] = source[index[0, c * rows * bucket + i]]
+            for f in range(frames):
+                packed_n[f, i] = near[f, index[0, i]]
 
         for k in range(1, rows):
-            tile_copy(c, f, k).start()
-        part = half if c == 0 else 1 - half
-        rec[f][pl.ds((part * rows + row) * bucket, bucket)] = packed[
-            c, f, pl.ds(row * bucket, bucket)
-        ]
+            tile_near(k).start()
+        own = pl.ds(row * bucket, bucket)
+        rec[:, pl.ds((half * rows + row) * bucket, bucket)] = packed_n[:, own]
+
+    def run_far(f):
+        for j in range(HALF):
+            far_copy(f, mine, j).wait_recv()
+        forward(f).wait_recv()
+
+        @pl.loop(0, rows * bucket)
+        def _(i):
+            packed_f[f, i] = far[f][index[0, rows * bucket + i]]
+
+        for k in range(1, rows):
+            tile_far(f, k).start()
+        own = pl.ds(row * bucket, bucket)
+        rec[f, pl.ds(((1 - half) * rows + row) * bucket, bucket)] = packed_f[f, own]
 
     for copy in small:
         copy.wait()
-    ws_copy.wait()
-    conv(start)
-    pl.semaphore_wait(barrier, slabs + rows - 2)
-    wt_copy.wait()
-
-    @pl.loop(0, slabs)
-    def _(k):
-        s = lax.rem(first + k, slabs)
-
-        @pl.when(k < slabs - 1)
-        def _():
-            conv(s)
-
-        mix(s)
-        send_slab(0, k)
-
-        @pl.when(k >= HALF)
-        def _():
-            send_slab(1, k)
-
-    @pl.loop(0, HALF)
-    def _(k):
-        send_slab(1, k)
-
     index_v[...] = index_row(tiles[...], rows, cap, bucket, group_tiles, row, half)
     index_copy = pltpu.make_async_copy(index_v, index, w_sem.at[6])
     index_copy.start()
+    ws_copy.wait()
+    conv(start)
     index_copy.wait()
-    pick_at = 2 * rows * bucket
-    full_at = pick_at + group_tiles
-
-    run_relay(0)
-    run_tiles(0, 0)
-    run_tiles(1, 0)
-    run_tiles(0, 1)
-    run_relay(1)
-    run_tiles(1, 1)
-
+    pl.semaphore_wait(barrier, slabs + rows - 2)
+    wt_copy.wait()
+
+    @pl.loop(0, steps)
+    def _(k):
+        z = lax.rem(origin + k, steps)
+
+        @pl.when(k < steps - 1)
+        def _():
+            conv(z)
+
+        mix(z)
+
+        @pl.when(k < 2)
+        def _():
+            x_copy(1, k).start()
+            for side_x in range(2):
+                far_copy(0, 2 * k + side_x, mine).start()
+
+        @pl.when(k >= 2)
+        def _():
+            x_copy(0, k - 2).start()
+            for side_x in range(2):
+                j = 2 * (k - 2) + side_x
+
+                @pl.when(j != mine)
+                def _():
+                    near_copy(j, mine).start()
+
+                @pl.when(j == mine)
+                def _():
+                    near[:, pl.ds(mine * BASE, BASE)] = lat[slab, :, 0:BASE]
+
+        @pl.when(k == 1)
+        def _():
+            merge_x(1)
+
+        @pl.when(k == 2)
+        def _():
+            merge_z_far()
+
+    for j in range(HALF):
+        far_copy(1, j, mine).start()
+    merge_x(0)
+    run_far(0)
+    run_near()
+    run_far(1)
+
+    for k in range(1, rows):
+        tile_near(k).wait_recv()
+        for f in range(frames):
+            tile_far(f, k).wait_recv()
+
+    @pl.loop(0, group_tiles)
+    def _(i):
+        for f in range(frames):
+            out[i, f] = rec[f, index[0, pick_at + i]]
+
+    for k in range(1, HALF):
+        near_copy(lax.rem(mine + k, HALF), mine).wait_send()
+    for c in range(2):
+        for place in range(2):
+            x_copy(c, place).wait_send()
+        z_copy(c).wait_send()
     for f in range(frames):
-        for c in range(2):
-            for k in range(1, rows):
-                tile_copy(c, f, k).wait_recv()
-
-        @pl.loop(0, group_tiles)
-        def _(i):
-            out[i, f] = rec[f][index[0, pick_at + i]]
-
-    for f in range(frames):
-        for k in range(1, HALF):
-            j = lax.rem(mine + k, HALF)
-            near_copy(f, j).wait_send()
-            relay_copy(f, j).wait_send()
         for j in range(HALF):
-            far_copy(f, j).wait_send()
+            far_copy(f, j, mine).wait_send()
         forward(f).wait_send()
-        for c in range(2):
-            for k in range(1, rows):
-                tile_copy(c, f, k).wait_send()
+        for k in range(1, rows):
+            tile_far(f, k).wait_send()
+    for k in range(1, rows):
+        tile_near(k).wait_send()
 
 
 def body_two_blocks(rows, slabs, pixels, slot_tile, w_space, b_space, w_time, b_time, gain):
@@ -595,12 +611,14 @@
     per_group = (cap + rows - 1) // rows
     bucket = per_group * 3
     area = pix_count // 4
-    count = frames * cap
-    height = count * area
+    span = 2 * frames
+    steps = slabs // 2
+    height = span * cap * area
     vmem = pl.BlockSpec(memory_space=pltpu.VMEM)
     hbm = pl.BlockSpec(memory_space=pl.ANY)
     bf16, f32 = jnp.bfloat16, jnp.float32
     dma = pltpu.SemaphoreType.DMA
+    arrivals = (HALF + 1) * BASE
 
     def held(*lead):
         return pltpu.VMEM(lead + (area, features), bf16)
@@ -611,7 +629,7 @@
         in_specs=[hbm] * 7,
         out_specs=vmem,
         scratch_shapes=[
-            pltpu.VMEM((slabs, cap, frames, pix_count, channels), bf16),
+            pltpu.VMEM((steps, cap, span, pix_count, channels), bf16),
             pltpu.VMEM((9 * channels, features), bf16),
             pltpu.VMEM((3, features, features), bf16),
             pltpu.VMEM((1, features), f32),
@@ -620,20 +638,20 @@
             pltpu.VMEM((1, slot_tile.shape[0]), jnp.int32),
             pltpu.VMEM((1, 128), jnp.int32),
             pltpu.SMEM((1, 128), jnp.int32),
-            pltpu.VMEM((2, channels // 128, count, 48, 128), f32),
+            pltpu.VMEM((2, channels // 128, span * cap, 48, 128), f32),
             pltpu.VMEM((height, 9 * channels), bf16),
-            pltpu.VMEM(((slabs + 1) * height, features), bf16),
+            pltpu.VMEM(((steps + 1) * height, features), bf16),
             held(slabs, frames, cap),
-            held(HALF * cap), held(HALF * cap),
-            held(HALF * BASE + BASE), held(HALF * BASE + BASE),
-            held(HALF * BASE), held(HALF * BASE),
+            held(frames, arrivals), held(arrivals), held(arrivals),
+            held(2, 2, frames, BASE), held(2, 2, frames, BASE),
+            held(2, frames, BASE), held(2, frames, BASE), held(2, frames, BASE),
             held(frames, BASE),
-            held(2, frames, rows * bucket),
-            held(2 * rows * bucket), held(2 * rows * bucket),
-            dma((slabs,)), dma((7,)),
-            dma((frames, slabs)), dma((frames, HALF)), dma((frames, HALF + 1)),
-            dma((frames, HALF)), dma((frames, HALF)), dma((frames,)),
-            dma((2, frames, rows - 1)), dma((2, frames, rows - 1)),
+            held(frames, rows * bucket), held(frames, rows * bucket),
+            held(frames, 2 * rows * bucket),
+            dma((steps,)), dma((7,)),
+            dma((HALF,)), dma((HALF,)), dma((frames, HALF)), dma((frames, HALF + 1)),
+            dma((2, 2)), dma((2, 2)), dma((2,)), dma((2,)), dma((frames,)),
+            dma((rows - 1,)), dma((rows - 1,)), dma((frames, rows - 1)), dma((frames, rows - 1)),
         ],
         compiler_params=pltpu.CompilerParams(
             collective_id=1, has_side_effects=True, vmem_limit_bytes=62 << 20

time: 49.7 us -> 51.9 us (1.044)
  the two profiles are of different devices: /device:TPU:17 before, /device:TPU:0 now
where the time goes in v3:
time: 51.9 us; the launch traced here: 51.3 us
  Pallas kernels  49.2 us (95%)
  local copies, waits for them, and re-layouts  2.09 us (4%)
    pallas_call x1, Pallas kernels, body_two_blocks(): pl.pallas_call(functools.partial(encode, rows, slabs, cap, bucket, group_...  49.2 us
    unnamed x1, local copies, waits for them, and re-layouts  2.09 us

profile of v3, /device:TPU:0, one launch (start us, length us, event | category | flops | bytes accessed | tf_op | source)
XLA Modules:
  0.0 51.3 jit_solution(3697572638715054124)
XLA Ops:
  0.0 49.2 %shard_map.73 = bf16[24,2,16,512]{3,2,1,0:T(8,128)(2,1)} custom-call(s32[1,192]{1,0:T(1,128)} %bitcast.9, bf16[6,16,64,256]{3,2,1,0:T(8,128)(2,1)} %pixels.1, bf16[2304,512]{1,0:T(8,128)(2,1)} %bitcast.5, f32[1,512]{1,0:T(1,128)} %bitcast.6, bf16[3,512,512]{2,1,0:T(8,128)(2,1)} %w_time.1, f32[1,512]{1,0:T(1,128)} %bitcast.7, f32[1,512]{1,0:T(1,128)} %bitcast.8), custom_call_target="tpu_custom_call" | custom-call | tf_op jit(solution)/shard_map/pallas_call | solution.py:626
  49.2 2.1 %copy.9 = bf16[24,2,16,512]{3,2,1,0:T(8,128)(2,1)} copy(bf16[24,2,16,512]{3,2,1,0:T(8,128)(2,1)} %shard_map.73) | data formatting | bytes 1572864

commit v4 on v3

--- a/solution.py
+++ b/solution.py
@@ -256,6 +256,7 @@
         dev = dev + jnp.where(inside >= k * cap, 1, 0)
     pos = inside - dev * cap
     came = jnp.where(pos < BASE, dev * BASE + pos, HALF * BASE + pos - BASE)
+    came = jnp.where(block == row * 2 + half, inside, came)
     mine = block == row * 2 + half
     other = block == row * 2 + 1 - half
     live = column >= 0
@@ -271,12 +272,15 @@
     )
     total = jnp.where(target == place, came, 0) + jnp.where(column == wanted, arrival, 0)
     full = mine & live & (pos == BASE)
-    for at, part_of in ((0, dev // 2), (1, dev % 2)):
-        total = total + jnp.where(full & (place == 2 * places + group_tiles + at), part_of, 0)
+    total = total + jnp.where(full & (place == 2 * places + group_tiles), dev, 0)
     limit = jnp.where(
-        place < 2 * places,
-        (HALF + 1) * BASE,
-        jnp.where(place < 2 * places + group_tiles, 2 * places, 2),
+        place < places,
+        width,
+        jnp.where(
+            place < 2 * places,
+            (HALF + 1) * BASE,
+            jnp.where(place < 2 * places + group_tiles, 2 * places, HALF),
+        ),
     )
     return jnp.minimum(jnp.sum(total, axis=0, keepdims=True), limit - 1)
 
@@ -286,24 +290,21 @@
     slot_tile, pixels, w_space, b_space_h, w_time, b_time_h, gain_h,
     out,
     pix, ws, wt, b_space, b_time, gain, tiles, index_v, index, plane, patch, spatial, lat,
-    near, far0, far1, x_near, x_far, z_near, z_far, z_out, forward_out,
+    near0, near1, far0, far1, relay0, relay1, forward_out,
     packed_n, packed_f, rec,
-    in_sem, w_sem, send_n, recv_n, send_f, recv_f, send_x, recv_x, send_z, recv_z,
+    in_sem, w_sem, send_n, recv_n, send_f, recv_f, send_x, recv_x,
     send_r, send_yn, recv_yn, send_yf, recv_yf,
 ):
     frames = 2
-    far = (far0, far1)
+    near = (near0, near1)
+    far, relay = (far0, far1), (relay0, relay1)
     f32, bf16 = jnp.float32, jnp.bfloat16
     row = lax.axis_index("tile")
     slab = lax.axis_index("tm")
     half = lax.div(slab, HALF)
     mine = lax.rem(slab, HALF)
-    x = lax.rem(slab, 2)
-    zl = lax.div(mine, 2)
     first = (1 - half) * HALF
     low = half * HALF
-    x_peer = slab + 1 - 2 * x
-    z_peer = slab + 2 - 4 * zl
     barrier = pltpu.get_barrier_semaphore()
     for k in range(1, slabs):
         pl.semaphore_signal(barrier, inc=1, device_id={"tm": lax.rem(slab + k, slabs)})
@@ -319,7 +320,14 @@
             pixels.at[:, pl.ds(z * span, span)], pix.at[z], in_sem.at[z]
         )
 
-    start = lax.rem(origin + steps - 1, steps)
+    begin = origin
+
+    def conv_at(c):
+        return lax.rem(begin + steps - 1 + c, steps)
+
+    def mix_at(k):
+        return lax.rem(begin + k, steps)
+
     small = [
         pltpu.make_async_copy(source, target, w_sem.at[2 + i])
         for i, (source, target) in enumerate(
@@ -328,16 +336,16 @@
     ]
     for copy in small:
         copy.start()
-    load(start).start()
+    load(conv_at(0)).start()
     ws_copy = pltpu.make_async_copy(w_space, ws, w_sem.at[0])
     ws_copy.start()
-    load(origin).start()
+    load(conv_at(1)).start()
     wt_copy = pltpu.make_async_copy(w_time, wt, w_sem.at[1])
     wt_copy.start()
 
-    @pl.loop(1, steps - 1)
-    def _(k):
-        load(lax.rem(origin + k, steps)).start()
+    @pl.loop(2, steps)
+    def _(c):
+        load(conv_at(c)).start()
 
     count = span * cap
     side = TILE_SIDE
@@ -400,13 +408,12 @@
         value = (mixed * scale * gain[...]).astype(bf16)
         lat[pl.ds(2 * z, 2)] = value.reshape(2, frames, cap, area, value.shape[-1])
 
-
-    def near_copy(j, source):
-        return pltpu.make_async_remote_copy(
-            src_ref=lat.at[low + j, :, pl.ds(0, BASE)],
-            dst_ref=near.at[:, pl.ds(source * BASE, BASE)],
-            send_sem=send_n.at[j],
-            recv_sem=recv_n.at[source],
+    def near_copy(f, j, source):
+        return pltpu.make_async_remote_copy(
+            src_ref=lat.at[low + j, f],
+            dst_ref=near[f].at[pl.ds(source * cap, cap)],
+            send_sem=send_n.at[f, j],
+            recv_sem=recv_n.at[f, source],
             device_id={"tm": low + j},
         )
 
@@ -419,24 +426,13 @@
             device_id={"tm": first + j},
         )
 
-
-    def x_copy(c, place):
-        s = (low if c == 0 else first) + 2 * place + 1 - x
-        return pltpu.make_async_remote_copy(
-            src_ref=lat.at[s, :, pl.ds(BASE, BASE)],
-            dst_ref=(x_near if c == 0 else x_far).at[place, x],
-            send_sem=send_x.at[c, place],
-            recv_sem=recv_x.at[c, place],
-            device_id={"tm": x_peer},
-        )
-
-    def z_copy(c):
-        return pltpu.make_async_remote_copy(
-            src_ref=z_out.at[c],
-            dst_ref=(z_near if c == 0 else z_far).at[zl],
-            send_sem=send_z.at[c],
-            recv_sem=recv_z.at[c],
-            device_id={"tm": z_peer},
+    def relay_copy(f, j, source):
+        return pltpu.make_async_remote_copy(
+            src_ref=lat.at[first + j, f, pl.ds(BASE, BASE)],
+            dst_ref=relay[f].at[source],
+            send_sem=send_x.at[f, j],
+            recv_sem=recv_x.at[f, source],
+            device_id={"tm": low + j},
         )
 
     def forward(f):
@@ -451,34 +447,48 @@
     pick_at = 2 * rows * bucket
     full_at = pick_at + group_tiles
 
-    def merge_x(c):
-        source, target, base = (x_near, z_near, low) if c == 0 else (x_far, z_far, first)
-        for place in range(2):
-            x_copy(c, place).wait_recv()
-            source[place, x] = lat[base + 2 * place + x, :, BASE:cap]
-        full_x = index[0, full_at + 1]
-        z_out[c] = source[1 - zl, full_x]
-        target[zl] = source[zl, full_x]
-        z_copy(c).start()
-
-    def merge_z_far():
-        z_copy(1).wait_recv()
-        forward_out[...] = z_far[index[0, full_at]]
-        for f in range(frames):
-            forward(f).start()
-
-    def merge_z_near():
-        z_copy(0).wait_recv()
-        near[:, HALF * BASE:] = z_near[index[0, full_at]]
-
-
-    def tile_near(k):
+    def send_near(f, place):
+        for side_x in range(2):
+            j = 2 * place + side_x
+
+            @pl.when(j != mine)
+            def _():
+                near_copy(f, j, mine).start()
+
+            @pl.when(j == mine)
+            def _():
+                near[f][pl.ds(mine * cap, cap)] = lat[slab, f]
+
+    def send_far(f, place):
+        for side_x in range(2):
+            far_copy(f, 2 * place + side_x, mine).start()
+
+    def send_relay(f, place):
+        for side_x in range(2):
+            j = 2 * place + side_x
+
+            @pl.when(j != mine)
+            def _():
+                relay_copy(f, j, mine).start()
+
+            @pl.when(j == mine)
+            def _():
+                relay[f][mine] = lat[first + mine, f, BASE:cap]
+
+    def run_relay(f):
+        for k in range(1, HALF):
+            relay_copy(f, mine, lax.rem(mine + k, HALF)).wait_recv()
+        forward_out[f] = relay[f][index[0, full_at]]
+        forward(f).start()
+
+
+    def tile_near(f, k):
         to = lax.rem(row + k, rows)
         return pltpu.make_async_remote_copy(
-            src_ref=packed_n.at[:, pl.ds(to * bucket, bucket)],
-            dst_ref=rec.at[:, pl.ds((half * rows + row) * bucket, bucket)],
-            send_sem=send_yn.at[k - 1],
-            recv_sem=recv_yn.at[k - 1],
+            src_ref=packed_n.at[f, pl.ds(to * bucket, bucket)],
+            dst_ref=rec.at[f, pl.ds((half * rows + row) * bucket, bucket)],
+            send_sem=send_yn.at[f, k - 1],
+            recv_sem=recv_yn.at[f, k - 1],
             device_id={"tile": to},
         )
 
@@ -492,20 +502,18 @@
             device_id={"tile": to},
         )
 
-    def run_near():
+    def run_near(f):
         for k in range(1, HALF):
-            near_copy(mine, lax.rem(mine + k, HALF)).wait_recv()
-        merge_z_near()
+            near_copy(f, mine, lax.rem(mine + k, HALF)).wait_recv()
 
         @pl.loop(0, rows * bucket)
         def _(i):
-            for f in range(frames):
-                packed_n[f, i] = near[f, index[0, i]]
+            packed_n[f, i] = near[f][index[0, i]]
 
         for k in range(1, rows):
-            tile_near(k).start()
+            tile_near(f, k).start()
         own = pl.ds(row * bucket, bucket)
-        rec[:, pl.ds((half * rows + row) * bucket, bucket)] = packed_n[:, own]
+        rec[f, pl.ds((half * rows + row) * bucket, bucket)] = packed_n[f, own]
 
     def run_far(f):
         for j in range(HALF):
@@ -527,59 +535,53 @@
     index_copy = pltpu.make_async_copy(index_v, index, w_sem.at[6])
     index_copy.start()
     ws_copy.wait()
-    conv(start)
+    conv(conv_at(0))
     index_copy.wait()
+    wt_copy.wait()
     pl.semaphore_wait(barrier, slabs + rows - 2)
-    wt_copy.wait()
 
     @pl.loop(0, steps)
     def _(k):
-        z = lax.rem(origin + k, steps)
-
         @pl.when(k < steps - 1)
         def _():
-            conv(z)
-
-        mix(z)
-
-        @pl.when(k < 2)
-        def _():
-            x_copy(1, k).start()
-            for side_x in range(2):
-                far_copy(0, 2 * k + side_x, mine).start()
-
-        @pl.when(k >= 2)
-        def _():
-            x_copy(0, k - 2).start()
-            for side_x in range(2):
-                j = 2 * (k - 2) + side_x
-
-                @pl.when(j != mine)
-                def _():
-                    near_copy(j, mine).start()
-
-                @pl.when(j == mine)
-                def _():
-                    near[:, pl.ds(mine * BASE, BASE)] = lat[slab, :, 0:BASE]
+            conv(conv_at(k + 1))
+
+        mix(mix_at(k))
+
+        @pl.when(k == 0)
+        def _():
+            send_relay(0, 0)
+            send_far(0, 0)
 
         @pl.when(k == 1)
         def _():
-            merge_x(1)
+            send_relay(0, 1)
+            send_far(0, 1)
 
         @pl.when(k == 2)
         def _():
-            merge_z_far()
-
-    for j in range(HALF):
-        far_copy(1, j, mine).start()
-    merge_x(0)
+            send_near(0, 0)
+            send_near(1, 0)
+
+        @pl.when(k == 3)
+        def _():
+            send_near(0, 1)
+            send_near(1, 1)
+
+    send_relay(1, 0)
+    send_relay(1, 1)
+    run_relay(0)
+    send_far(1, 0)
+    send_far(1, 1)
+    run_near(0)
     run_far(0)
-    run_near()
+    run_relay(1)
+    run_near(1)
     run_far(1)
 
     for k in range(1, rows):
-        tile_near(k).wait_recv()
         for f in range(frames):
+            tile_near(f, k).wait_recv()
             tile_far(f, k).wait_recv()
 
     @pl.loop(0, group_tiles)
@@ -588,19 +590,19 @@
             out[i, f] = rec[f, index[0, pick_at + i]]
 
     for k in range(1, HALF):
-        near_copy(lax.rem(mine + k, HALF), mine).wait_send()
-    for c in range(2):
-        for place in range(2):
-            x_copy(c, place).wait_send()
-        z_copy(c).wait_send()
+        for f in range(frames):
+            near_copy(f, lax.rem(mine + k, HALF), mine).wait_send()
     for f in range(frames):
         for j in range(HALF):
             far_copy(f, j, mine).wait_send()
+        for k in range(1, HALF):
+            relay_copy(f, lax.rem(mine + k, HALF), mine).wait_send()
         forward(f).wait_send()
         for k in range(1, rows):
             tile_far(f, k).wait_send()
     for k in range(1, rows):
-        tile_near(k).wait_send()
+        for f in range(frames):
+            tile_near(f, k).wait_send()
 
 
 def body_two_blocks(rows, slabs, pixels, slot_tile, w_space, b_space, w_time, b_time, gain):
@@ -642,16 +644,14 @@
             pltpu.VMEM((height, 9 * channels), bf16),
             pltpu.VMEM(((steps + 1) * height, features), bf16),
             held(slabs, frames, cap),
-            held(frames, arrivals), held(arrivals), held(arrivals),
-            held(2, 2, frames, BASE), held(2, 2, frames, BASE),
-            held(2, frames, BASE), held(2, frames, BASE), held(2, frames, BASE),
-            held(frames, BASE),
+            held(HALF * cap), held(HALF * cap), held(arrivals), held(arrivals),
+            held(HALF, BASE), held(HALF, BASE), held(frames, BASE),
             held(frames, rows * bucket), held(frames, rows * bucket),
             held(frames, 2 * rows * bucket),
             dma((steps,)), dma((7,)),
-            dma((HALF,)), dma((HALF,)), dma((frames, HALF)), dma((frames, HALF + 1)),
-            dma((2, 2)), dma((2, 2)), dma((2,)), dma((2,)), dma((frames,)),
-            dma((rows - 1,)), dma((rows - 1,)), dma((frames, rows - 1)), dma((frames, rows - 1)),
+            dma((frames, HALF)), dma((frames, HALF)), dma((frames, HALF)), dma((frames, HALF + 1)),
+            dma((frames, HALF)), dma((frames, HALF)), dma((frames,)),
+            dma((frames, rows - 1)), dma((frames, rows - 1)), dma((frames, rows - 1)), dma((frames, rows - 1)),
         ],
         compiler_params=pltpu.CompilerParams(
             collective_id=1, has_side_effects=True, vmem_limit_bytes=62 << 20

time: 51.9 us -> 47.6 us (0.917)
  the two profiles are of different devices: /device:TPU:0 before, /device:TPU:27 now
where the time goes in v4:
time: 47.6 us; the launch traced here: 47.4 us
  Pallas kernels  45.3 us (95%)
  local copies, waits for them, and re-layouts  2.09 us (4%)
    pallas_call x1, Pallas kernels, body_two_blocks(): pl.pallas_call(functools.partial(encode, rows, slabs, cap, bucket, group_...  45.3 us
    unnamed x1, local copies, waits for them, and re-layouts  2.09 us

profile of v4, /device:TPU:27, one launch (start us, length us, event | category | flops | bytes accessed | tf_op | source)
XLA Modules:
  0.0 47.4 jit_solution(17839354585409876295)
XLA Ops:
  0.0 45.3 %shard_map.73 = bf16[24,2,16,512]{3,2,1,0:T(8,128)(2,1)} custom-call(s32[1,192]{1,0:T(1,128)} %bitcast.9, bf16[6,16,64,256]{3,2,1,0:T(8,128)(2,1)} %pixels.1, bf16[2304,512]{1,0:T(8,128)(2,1)} %bitcast.5, f32[1,512]{1,0:T(1,128)} %bitcast.6, bf16[3,512,512]{2,1,0:T(8,128)(2,1)} %w_time.1, f32[1,512]{1,0:T(1,128)} %bitcast.7, f32[1,512]{1,0:T(1,128)} %bitcast.8), custom_call_target="tpu_custom_call" | custom-call | tf_op jit(solution)/shard_map/pallas_call | solution.py:628
  45.4 2.1 %copy.9 = bf16[24,2,16,512]{3,2,1,0:T(8,128)(2,1)} copy(bf16[24,2,16,512]{3,2,1,0:T(8,128)(2,1)} %shard_map.73) | data formatting | bytes 1572864

commit v5 on v4

--- a/solution.py
+++ b/solution.py
@@ -286,18 +286,21 @@
 
 
 def encode(
-    rows, slabs, cap, bucket, group_tiles,
+    rows, slabs, cap, bucket, group_tiles, pieces,
     slot_tile, pixels, w_space, b_space_h, w_time, b_time_h, gain_h,
     out,
-    pix, ws, wt, b_space, b_time, gain, tiles, index_v, index, plane, patch, spatial, lat,
-    near0, near1, far0, far1, relay0, relay1, forward_out,
-    packed_n, packed_f, rec,
-    in_sem, w_sem, send_n, recv_n, send_f, recv_f, send_x, recv_x,
-    send_r, send_yn, recv_yn, send_yf, recv_yf,
+    pix, ws, wt, b_space, b_time, gain, tiles, index_v, index, plane, spatial, lat,
+    *landing,
 ):
     frames = 2
-    near = (near0, near1)
-    far, relay = (far0, far1), (relay0, relay1)
+    near, far, relay = (landing[i * frames * pieces:(i + 1) * frames * pieces] for i in range(3))
+    (
+        forward_out, packed_n, packed_f, rec,
+        in_sem, w_sem, send_n, recv_n, send_f, recv_f, send_x, recv_x,
+        send_r, send_yn, recv_yn, send_yf, recv_yf,
+    ) = landing[3 * frames * pieces:]
+    parts = frames * pieces
+    breadth = lat.shape[-1]
     f32, bf16 = jnp.float32, jnp.bfloat16
     row = lax.axis_index("tile")
     slab = lax.axis_index("tm")
@@ -315,18 +318,23 @@
     span = 2 * frames
     origin = lax.div(first, 2)
 
+    def load_frame(z, f):
+        return pltpu.make_async_copy(
+            pixels.at[:, z * span + f], pix.at[z, f], in_sem.at[z, f]
+        )
+
     def load(z):
-        return pltpu.make_async_copy(
-            pixels.at[:, pl.ds(z * span, span)], pix.at[z], in_sem.at[z]
-        )
-
-    begin = origin
+        for f in range(span):
+            load_frame(z, f).start()
 
     def conv_at(c):
-        return lax.rem(begin + steps - 1 + c, steps)
+        return lax.rem(c + 1 - half, steps)
 
     def mix_at(k):
-        return lax.rem(begin + k, steps)
+        return lax.rem(origin + k, steps)
+
+    def conv_before(k):
+        return jnp.minimum(k + 2 - half, steps)
 
     small = [
         pltpu.make_async_copy(source, target, w_sem.at[2 + i])
@@ -336,16 +344,16 @@
     ]
     for copy in small:
         copy.start()
-    load(conv_at(0)).start()
+    load(conv_at(0))
     ws_copy = pltpu.make_async_copy(w_space, ws, w_sem.at[0])
     ws_copy.start()
-    load(conv_at(1)).start()
+    load(conv_at(1))
     wt_copy = pltpu.make_async_copy(w_time, wt, w_sem.at[1])
     wt_copy.start()
 
     @pl.loop(2, steps)
     def _(c):
-        load(conv_at(c)).start()
+        load(conv_at(c))
 
     count = span * cap
     side = TILE_SIDE
@@ -353,45 +361,34 @@
     area = out_side * out_side
     height = count * area
     step_rows = height // span
-    channels = patch.shape[1] // 9
+    channels = pix.shape[-1]
     lanes = plane.shape[-1]
     for piece in range(channels // lanes):
         plane[1, piece, :, 8:16] = jnp.zeros((count, 8, lanes), f32)
     spatial[height - 2 * step_rows:height] = jnp.zeros((2 * step_rows, spatial.shape[1]), bf16)
-    edge = lax.rem(lax.broadcasted_iota(jnp.int32, (area, lanes), 0), out_side) == 0
+    edge = lax.rem(lax.broadcasted_iota(jnp.int32, (count, area, lanes), 1), out_side) == 0
 
     def conv(z):
-        load(z).wait()
-
-        @pl.loop(0, cap)
-        def _(p):
-            for f in range(span):
-                image = f * cap + p
-                value = pix[z, p, f].astype(f32).reshape(out_side, 2, side, channels)
-                for parity in range(2):
-                    rows_of = value[:, parity].reshape(out_side * side, channels)
-                    for piece in range(channels // lanes):
-                        plane[parity, piece, image, 16:48] = rows_of[
-                            :, piece * lanes:(piece + 1) * lanes
-                        ]
-            for f in range(span):
-                image = f * cap + p
-                for a in range(3):
-                    parity, base = ((1, 8), (0, 16), (1, 16))[a]
-                    for b in range(3):
-                        for piece in range(channels // lanes):
-                            taken = plane[
-                                parity, piece, image, pl.ds(base + b - 1, area, stride=2)
-                            ]
-                            if b == 0:
-                                taken = jnp.where(edge, 0.0, taken)
-                            at = (3 * a + b) * channels + piece * lanes
-                            patch[
-                                pl.ds(pl.multiple_of(image * area, area), area),
-                                at:at + lanes,
-                            ] = taken.astype(bf16)
-
-        total = jnp.dot(patch[...], ws[...], preferred_element_type=f32) + b_space[...]
+        for f in range(span):
+            load_frame(z, f).wait()
+
+        value = pix[z].astype(f32).reshape(count, out_side, 2, side, channels)
+        for parity in range(2):
+            rows_of = value[:, :, parity].reshape(count, out_side * side, channels)
+            for piece in range(channels // lanes):
+                plane[parity, piece, :, 16:48] = rows_of[:, :, piece * lanes:(piece + 1) * lanes]
+
+        parts = []
+        for a in range(3):
+            parity, base = ((1, 8), (0, 16), (1, 16))[a]
+            for b in range(3):
+                for piece in range(channels // lanes):
+                    taken = plane[parity, piece, :, pl.ds(base + b - 1, area, stride=2)]
+                    if b == 0:
+                        taken = jnp.where(edge, 0.0, taken)
+                    parts.append(taken.reshape(height, lanes).astype(bf16))
+        patch = jnp.concatenate(parts, axis=1)
+        total = jnp.dot(patch, ws[...], preferred_element_type=f32) + b_space[...]
         active = total / (1.0 + jnp.exp(-total))
         spatial[pl.ds(pl.multiple_of((z + 1) * height, height), height)] = active.astype(bf16)
 
@@ -406,128 +403,131 @@
             )
         scale = lax.rsqrt(jnp.mean(mixed * mixed, axis=-1, keepdims=True) + 1e-06)
         value = (mixed * scale * gain[...]).astype(bf16)
-        lat[pl.ds(2 * z, 2)] = value.reshape(2, frames, cap, area, value.shape[-1])
-
-    def near_copy(f, j, source):
-        return pltpu.make_async_remote_copy(
-            src_ref=lat.at[low + j, f],
-            dst_ref=near[f].at[pl.ds(source * cap, cap)],
-            send_sem=send_n.at[f, j],
-            recv_sem=recv_n.at[f, source],
+        for h in range(pieces):
+            lat[h, pl.ds(2 * z, 2)] = value[:, h * breadth:(h + 1) * breadth].reshape(
+                2, frames, cap, area, breadth
+            )
+
+    def near_copy(q, j, source):
+        return pltpu.make_async_remote_copy(
+            src_ref=lat.at[q % pieces, low + j, q // pieces],
+            dst_ref=near[q].at[pl.ds(source * cap, cap)],
+            send_sem=send_n.at[q, j],
+            recv_sem=recv_n.at[q, source],
             device_id={"tm": low + j},
         )
 
-    def far_copy(f, j, source):
-        return pltpu.make_async_remote_copy(
-            src_ref=lat.at[first + j, f, pl.ds(0, BASE)],
-            dst_ref=far[f].at[pl.ds(source * BASE, BASE)],
-            send_sem=send_f.at[f, j],
-            recv_sem=recv_f.at[f, source],
+    def far_copy(q, j, source):
+        return pltpu.make_async_remote_copy(
+            src_ref=lat.at[q % pieces, first + j, q // pieces, pl.ds(0, BASE)],
+            dst_ref=far[q].at[pl.ds(source * BASE, BASE)],
+            send_sem=send_f.at[q, j],
+            recv_sem=recv_f.at[q, source],
             device_id={"tm": first + j},
         )
 
-    def relay_copy(f, j, source):
-        return pltpu.make_async_remote_copy(
-            src_ref=lat.at[first + j, f, pl.ds(BASE, BASE)],
-            dst_ref=relay[f].at[source],
-            send_sem=send_x.at[f, j],
-            recv_sem=recv_x.at[f, source],
+    def relay_copy(q, j, source):
+        return pltpu.make_async_remote_copy(
+            src_ref=lat.at[q % pieces, first + j, q // pieces, pl.ds(BASE, BASE)],
+            dst_ref=relay[q].at[source],
+            send_sem=send_x.at[q, j],
+            recv_sem=recv_x.at[q, source],
             device_id={"tm": low + j},
         )
 
-    def forward(f):
-        return pltpu.make_async_remote_copy(
-            src_ref=forward_out.at[f],
-            dst_ref=far[f].at[pl.ds(HALF * BASE, BASE)],
-            send_sem=send_r.at[f],
-            recv_sem=recv_f.at[f, HALF],
+    def forward(q):
+        return pltpu.make_async_remote_copy(
+            src_ref=forward_out.at[q],
+            dst_ref=far[q].at[pl.ds(HALF * BASE, BASE)],
+            send_sem=send_r.at[q],
+            recv_sem=recv_f.at[q, HALF],
             device_id={"tm": first + mine},
         )
 
     pick_at = 2 * rows * bucket
     full_at = pick_at + group_tiles
 
-    def send_near(f, place):
+    def send_near(q, place):
         for side_x in range(2):
             j = 2 * place + side_x
 
             @pl.when(j != mine)
             def _():
-                near_copy(f, j, mine).start()
+                near_copy(q, j, mine).start()
 
             @pl.when(j == mine)
             def _():
-                near[f][pl.ds(mine * cap, cap)] = lat[slab, f]
-
-    def send_far(f, place):
+                near[q][pl.ds(mine * cap, cap)] = lat[q % pieces, slab, q // pieces]
+
+    def send_far(q, place):
         for side_x in range(2):
-            far_copy(f, 2 * place + side_x, mine).start()
-
-    def send_relay(f, place):
+            far_copy(q, 2 * place + side_x, mine).start()
+
+    def send_relay(q, place):
         for side_x in range(2):
             j = 2 * place + side_x
 
             @pl.when(j != mine)
             def _():
-                relay_copy(f, j, mine).start()
+                relay_copy(q, j, mine).start()
 
             @pl.when(j == mine)
             def _():
-                relay[f][mine] = lat[first + mine, f, BASE:cap]
-
-    def run_relay(f):
+                relay[q][mine] = lat[q % pieces, first + mine, q // pieces, BASE:cap]
+
+    def run_relay(q):
         for k in range(1, HALF):
-            relay_copy(f, mine, lax.rem(mine + k, HALF)).wait_recv()
-        forward_out[f] = relay[f][index[0, full_at]]
-        forward(f).start()
-
-
-    def tile_near(f, k):
+            relay_copy(q, mine, lax.rem(mine + k, HALF)).wait_recv()
+        forward_out[q] = relay[q][index[0, full_at]]
+        forward(q).start()
+
+
+    def tile_near(q, k):
         to = lax.rem(row + k, rows)
         return pltpu.make_async_remote_copy(
-            src_ref=packed_n.at[f, pl.ds(to * bucket, bucket)],
-            dst_ref=rec.at[f, pl.ds((half * rows + row) * bucket, bucket)],
-            send_sem=send_yn.at[f, k - 1],
-            recv_sem=recv_yn.at[f, k - 1],
+            src_ref=packed_n.at[q, pl.ds(to * bucket, bucket)],
+            dst_ref=rec.at[q, pl.ds((half * rows + row) * bucket, bucket)],
+            send_sem=send_yn.at[q, k - 1],
+            recv_sem=recv_yn.at[q, k - 1],
             device_id={"tile": to},
         )
 
-    def tile_far(f, k):
+    def tile_far(q, k):
         to = lax.rem(row + k, rows)
         return pltpu.make_async_remote_copy(
-            src_ref=packed_f.at[f, pl.ds(to * bucket, bucket)],
-            dst_ref=rec.at[f, pl.ds(((1 - half) * rows + row) * bucket, bucket)],
-            send_sem=send_yf.at[f, k - 1],
-            recv_sem=recv_yf.at[f, k - 1],
+            src_ref=packed_f.at[q, pl.ds(to * bucket, bucket)],
+            dst_ref=rec.at[q, pl.ds(((1 - half) * rows + row) * bucket, bucket)],
+            send_sem=send_yf.at[q, k - 1],
+            recv_sem=recv_yf.at[q, k - 1],
             device_id={"tile": to},
         )
 
-    def run_near(f):
+    def run_near(q):
         for k in range(1, HALF):
-            near_copy(f, mine, lax.rem(mine + k, HALF)).wait_recv()
+            near_copy(q, mine, lax.rem(mine + k, HALF)).wait_recv()
 
         @pl.loop(0, rows * bucket)
         def _(i):
-            packed_n[f, i] = near[f][index[0, i]]
+            packed_n[q, i] = near[q][index[0, i]]
 
         for k in range(1, rows):
-            tile_near(f, k).start()
+            tile_near(q, k).start()
         own = pl.ds(row * bucket, bucket)
-        rec[f, pl.ds((half * rows + row) * bucket, bucket)] = packed_n[f, own]
-
-    def run_far(f):
+        rec[q, pl.ds((half * rows + row) * bucket, bucket)] = packed_n[q, own]
+
+    def run_far(q):
         for j in range(HALF):
-            far_copy(f, mine, j).wait_recv()
-        forward(f).wait_recv()
+            far_copy(q, mine, j).wait_recv()
+        forward(q).wait_recv()
 
         @pl.loop(0, rows * bucket)
         def _(i):
-            packed_f[f, i] = far[f][index[0, rows * bucket + i]]
+            packed_f[q, i] = far[q][index[0, rows * bucket + i]]
 
         for k in range(1, rows):
-            tile_far(f, k).start()
+            tile_far(q, k).start()
         own = pl.ds(row * bucket, bucket)
-        rec[f, pl.ds(((1 - half) * rows + row) * bucket, bucket)] = packed_f[f, own]
+        rec[q, pl.ds(((1 - half) * rows + row) * bucket, bucket)] = packed_f[q, own]
 
     for copy in small:
         copy.wait()
@@ -542,21 +542,25 @@
 
     @pl.loop(0, steps)
     def _(k):
-        @pl.when(k < steps - 1)
-        def _():
-            conv(conv_at(k + 1))
+        @pl.loop(jnp.where(k == 0, 1, conv_before(k - 1)), conv_before(k))
+        def _(c):
+            conv(conv_at(c))
 
         mix(mix_at(k))
 
         @pl.when(k == 0)
         def _():
             send_relay(0, 0)
+            send_relay(1, 0)
             send_far(0, 0)
+            send_far(1, 0)
 
         @pl.when(k == 1)
         def _():
             send_relay(0, 1)
+            send_relay(1, 1)
             send_far(0, 1)
+            send_far(1, 1)
 
         @pl.when(k == 2)
         def _():
@@ -567,42 +571,53 @@
         def _():
             send_near(0, 1)
             send_near(1, 1)
-
-    send_relay(1, 0)
-    send_relay(1, 1)
-    run_relay(0)
-    send_far(1, 0)
-    send_far(1, 1)
+            run_relay(0)
+            run_relay(1)
+
+    send_near(2, 0)
+    send_near(2, 1)
+    send_relay(2, 0)
+    send_relay(2, 1)
+    send_far(2, 0)
+    send_far(2, 1)
+    send_near(3, 0)
+    send_near(3, 1)
+    send_relay(3, 0)
+    send_relay(3, 1)
+    send_far(3, 0)
+    send_far(3, 1)
     run_near(0)
+    run_near(1)
     run_far(0)
-    run_relay(1)
-    run_near(1)
     run_far(1)
+    run_near(2)
+    run_relay(2)
+    run_far(2)
+    run_near(3)
+    run_relay(3)
+    run_far(3)
 
     for k in range(1, rows):
-        for f in range(frames):
-            tile_near(f, k).wait_recv()
-            tile_far(f, k).wait_recv()
+        for q in range(parts):
+            tile_near(q, k).wait_recv()
+            tile_far(q, k).wait_recv()
 
     @pl.loop(0, group_tiles)
     def _(i):
-        for f in range(frames):
-            out[i, f] = rec[f, index[0, pick_at + i]]
-
-    for k in range(1, HALF):
-        for f in range(frames):
-            near_copy(f, lax.rem(mine + k, HALF), mine).wait_send()
-    for f in range(frames):
+        for q in range(parts):
+            h = q % pieces
+            out[i, q // pieces, :, h * breadth:(h + 1) * breadth] = rec[q, index[0, pick_at + i]]
+
+    for q in range(parts):
+        for k in range(1, HALF):
+            near_copy(q, lax.rem(mine + k, HALF), mine).wait_send()
+            relay_copy(q, lax.rem(mine + k, HALF), mine).wait_send()
         for j in range(HALF):
-            far_copy(f, j, mine).wait_send()
-        for k in range(1, HALF):
-            relay_copy(f, lax.rem(mine + k, HALF), mine).wait_send()
-        forward(f).wait_send()
+            far_copy(q, j, mine).wait_send()
+        forward(q).wait_send()
         for k in range(1, rows):
-            tile_far(f, k).wait_send()
-    for k in range(1, rows):
-        for f in range(frames):
-            tile_near(f, k).wait_send()
+            tile_far(q, k).wait_send()
+            tile_near(q, k).wait_send()
 
 
 def body_two_blocks(rows, slabs, pixels, slot_tile, w_space, b_space, w_time, b_time, gain):
@@ -621,17 +636,19 @@
     bf16, f32 = jnp.bfloat16, jnp.float32
     dma = pltpu.SemaphoreType.DMA
     arrivals = (HALF + 1) * BASE
+    pieces = 2
+    parts = frames * pieces
 
     def held(*lead):
-        return pltpu.VMEM(lead + (area, features), bf16)
+        return pltpu.VMEM(lead + (area, features // pieces), bf16)
 
     return pl.pallas_call(
-        functools.partial(encode, rows, slabs, cap, bucket, group_tiles),
+        functools.partial(encode, rows, slabs, cap, bucket, group_tiles, pieces),
         out_shape=jax.ShapeDtypeStruct((group_tiles, frames, area, features), bf16),
         in_specs=[hbm] * 7,
         out_specs=vmem,
         scratch_shapes=[
-            pltpu.VMEM((steps, cap, span, pix_count, channels), bf16),
+            pltpu.VMEM((steps, span, cap, pix_count, channels), bf16),
             pltpu.VMEM((9 * channels, features), bf16),
             pltpu.VMEM((3, features, features), bf16),
             pltpu.VMEM((1, features), f32),
@@ -641,17 +658,15 @@
             pltpu.VMEM((1, 128), jnp.int32),
             pltpu.SMEM((1, 128), jnp.int32),
             pltpu.VMEM((2, channels // 128, span * cap, 48, 128), f32),
-            pltpu.VMEM((height, 9 * channels), bf16),
             pltpu.VMEM(((steps + 1) * height, features), bf16),
-            held(slabs, frames, cap),
-            held(HALF * cap), held(HALF * cap), held(arrivals), held(arrivals),
-            held(HALF, BASE), held(HALF, BASE), held(frames, BASE),
-            held(frames, rows * bucket), held(frames, rows * bucket),
-            held(frames, 2 * rows * bucket),
-            dma((steps,)), dma((7,)),
-            dma((frames, HALF)), dma((frames, HALF)), dma((frames, HALF)), dma((frames, HALF + 1)),
-            dma((frames, HALF)), dma((frames, HALF)), dma((frames,)),
-            dma((frames, rows - 1)), dma((frames, rows - 1)), dma((frames, rows - 1)), dma((frames, rows - 1)),
+            held(pieces, slabs, frames, cap),
+            *[held(HALF * cap)] * parts, *[held(arrivals)] * parts, *[held(HALF, BASE)] * parts,
+            held(parts, BASE),
+            held(parts, rows * bucket), held(parts, rows * bucket), held(parts, 2 * rows * bucket),
+            dma((steps, span)), dma((7,)),
+            dma((parts, HALF)), dma((parts, HALF)), dma((parts, HALF)), dma((parts, HALF + 1)),
+            dma((parts, HALF)), dma((parts, HALF)), dma((parts,)),
+            dma((parts, rows - 1)), dma((parts, rows - 1)), dma((parts, rows - 1)), dma((parts, rows - 1)),
         ],
         compiler_params=pltpu.CompilerParams(
             collective_id=1, has_side_effects=True, vmem_limit_bytes=62 << 20

time: 47.6 us -> 45.3 us (0.952)
  the two profiles are of different devices: /device:TPU:27 before, /device:TPU:0 now
where the time goes in v5:
time: 45.3 us; the launch traced here: 44.9 us
  Pallas kernels  42.8 us (94%)
  local copies, waits for them, and re-layouts  2.09 us (5%)
    pallas_call x1, Pallas kernels, body_two_blocks(): pl.pallas_call(functools.partial(encode, rows, slabs, cap, bucket, group_...  42.8 us
    unnamed x1, local copies, waits for them, and re-layouts  2.09 us

profile of v5, /device:TPU:0, one launch (start us, length us, event | category | flops | bytes accessed | tf_op | source)
XLA Modules:
  0.0 44.9 jit_solution(5440078367275966407)
XLA Ops:
  0.0 42.8 %shard_map.73 = bf16[24,2,16,512]{3,2,1,0:T(8,128)(2,1)} custom-call(s32[1,192]{1,0:T(1,128)} %bitcast.9, bf16[6,16,64,256]{3,2,1,0:T(8,128)(2,1)} %pixels.1, bf16[2304,512]{1,0:T(8,128)(2,1)} %bitcast.5, f32[1,512]{1,0:T(1,128)} %bitcast.6, bf16[3,512,512]{2,1,0:T(8,128)(2,1)} %w_time.1, f32[1,512]{1,0:T(1,128)} %bitcast.7, f32[1,512]{1,0:T(1,128)} %bitcast.8), custom_call_target="tpu_custom_call" | custom-call | tf_op jit(solution)/shard_map/pallas_call | solution.py:645
  42.8 2.1 %copy.9 = bf16[24,2,16,512]{3,2,1,0:T(8,128)(2,1)} copy(bf16[24,2,16,512]{3,2,1,0:T(8,128)(2,1)} %shard_map.73) | data formatting | bytes 1572864

commit v6 on v5

--- a/solution.py
+++ b/solution.py
@@ -109,7 +109,7 @@
         for k in range(1, slabs):
             copy1(f, k).wait_recv()
 
-        @pl.loop(0, rows * bucket)
+        @pl.loop(0, rows * bucket, unroll=8)
         def _(i):
             out2[f, i] = got1[f][send_idx[i]]
 
@@ -123,7 +123,7 @@
         for k in range(1, rows):
             copy2(f, k).wait_recv()
 
-        @pl.loop(0, group_tiles)
+        @pl.loop(0, group_tiles, unroll=4)
         def _(i):
             feats[f, i] = got2[f][pick_idx[i]]
 
@@ -293,12 +293,14 @@
     *landing,
 ):
     frames = 2
-    near, far, relay = (landing[i * frames * pieces:(i + 1) * frames * pieces] for i in range(3))
+    near, far, relay, rec = (
+        landing[i * frames * pieces:(i + 1) * frames * pieces] for i in range(4)
+    )
     (
-        forward_out, packed_n, packed_f, rec,
+        forward_out, packed_n, packed_f,
         in_sem, w_sem, send_n, recv_n, send_f, recv_f, send_x, recv_x,
         send_r, send_yn, recv_yn, send_yf, recv_yf,
-    ) = landing[3 * frames * pieces:]
+    ) = landing[4 * frames * pieces:]
     parts = frames * pieces
     breadth = lat.shape[-1]
     f32, bf16 = jnp.float32, jnp.bfloat16
@@ -486,7 +488,7 @@
         to = lax.rem(row + k, rows)
         return pltpu.make_async_remote_copy(
             src_ref=packed_n.at[q, pl.ds(to * bucket, bucket)],
-            dst_ref=rec.at[q, pl.ds((half * rows + row) * bucket, bucket)],
+            dst_ref=rec[q].at[pl.ds((half * rows + row) * bucket, bucket)],
             send_sem=send_yn.at[q, k - 1],
             recv_sem=recv_yn.at[q, k - 1],
             device_id={"tile": to},
@@ -496,38 +498,40 @@
         to = lax.rem(row + k, rows)
         return pltpu.make_async_remote_copy(
             src_ref=packed_f.at[q, pl.ds(to * bucket, bucket)],
-            dst_ref=rec.at[q, pl.ds(((1 - half) * rows + row) * bucket, bucket)],
+            dst_ref=rec[q].at[pl.ds(((1 - half) * rows + row) * bucket, bucket)],
             send_sem=send_yf.at[q, k - 1],
             recv_sem=recv_yf.at[q, k - 1],
             device_id={"tile": to},
         )
 
+    tile_order = sorted(range(1, rows), key=lambda k: k % 2)
+
     def run_near(q):
         for k in range(1, HALF):
             near_copy(q, mine, lax.rem(mine + k, HALF)).wait_recv()
 
-        @pl.loop(0, rows * bucket)
+        @pl.loop(0, rows * bucket, unroll=8)
         def _(i):
             packed_n[q, i] = near[q][index[0, i]]
 
-        for k in range(1, rows):
+        for k in tile_order:
             tile_near(q, k).start()
         own = pl.ds(row * bucket, bucket)
-        rec[q, pl.ds((half * rows + row) * bucket, bucket)] = packed_n[q, own]
+        rec[q][pl.ds((half * rows + row) * bucket, bucket)] = packed_n[q, own]
 
     def run_far(q):
         for j in range(HALF):
             far_copy(q, mine, j).wait_recv()
         forward(q).wait_recv()
 
-        @pl.loop(0, rows * bucket)
+        @pl.loop(0, rows * bucket, unroll=8)
         def _(i):
             packed_f[q, i] = far[q][index[0, rows * bucket + i]]
 
-        for k in range(1, rows):
+        for k in tile_order:
             tile_far(q, k).start()
         own = pl.ds(row * bucket, bucket)
-        rec[q, pl.ds(((1 - half) * rows + row) * bucket, bucket)] = packed_f[q, own]
+        rec[q][pl.ds(((1 - half) * rows + row) * bucket, bucket)] = packed_f[q, own]
 
     for copy in small:
         copy.wait()
@@ -580,10 +584,10 @@
     send_relay(2, 1)
     send_far(2, 0)
     send_far(2, 1)
+    send_relay(3, 0)
+    send_relay(3, 1)
     send_near(3, 0)
     send_near(3, 1)
-    send_relay(3, 0)
-    send_relay(3, 1)
     send_far(3, 0)
     send_far(3, 1)
     run_near(0)
@@ -593,20 +597,19 @@
     run_near(2)
     run_relay(2)
     run_far(2)
+    run_relay(3)
     run_near(3)
-    run_relay(3)
     run_far(3)
 
-    for k in range(1, rows):
-        for q in range(parts):
+    for q in range(parts):
+        for k in range(1, rows):
             tile_near(q, k).wait_recv()
             tile_far(q, k).wait_recv()
 
-    @pl.loop(0, group_tiles)
-    def _(i):
-        for q in range(parts):
+        @pl.loop(0, group_tiles, unroll=4)
+        def _(i):
             h = q % pieces
-            out[i, q // pieces, :, h * breadth:(h + 1) * breadth] = rec[q, index[0, pick_at + i]]
+            out[i, q // pieces, :, h * breadth:(h + 1) * breadth] = rec[q][index[0, pick_at + i]]
 
     for q in range(parts):
         for k in range(1, HALF):
@@ -661,8 +664,9 @@
             pltpu.VMEM(((steps + 1) * height, features), bf16),
             held(pieces, slabs, frames, cap),
             *[held(HALF * cap)] * parts, *[held(arrivals)] * parts, *[held(HALF, BASE)] * parts,
+            *[held(2 * rows * bucket)] * parts,
             held(parts, BASE),
-            held(parts, rows * bucket), held(parts, rows * bucket), held(parts, 2 * rows * bucket),
+            held(parts, rows * bucket), held(parts, rows * bucket),
             dma((steps, span)), dma((7,)),
             dma((parts, HALF)), dma((parts, HALF)), dma((parts, HALF)), dma((parts, HALF + 1)),
             dma((parts, HALF)), dma((parts, HALF)), dma((parts,)),

time: 45.3 us -> 45 us (level)
  no operation moved by 1% of the time
where the time goes in v6:
time: 45 us; the launch traced here: 44.6 us
  Pallas kernels  42.5 us (94%)
  local copies, waits for them, and re-layouts  2.09 us (5%)
    pallas_call x1, Pallas kernels, body_two_blocks(): pl.pallas_call(functools.partial(encode, rows, slabs, cap, bucket, group_...  42.5 us
    unnamed x1, local copies, waits for them, and re-layouts  2.09 us

profile of v6, /device:TPU:0, one launch (start us, length us, event | category | flops | bytes accessed | tf_op | source)
XLA Modules:
  0.0 44.6 jit_solution(18010850968898927538)
XLA Ops:
  0.0 42.5 %shard_map.73 = bf16[24,2,16,512]{3,2,1,0:T(8,128)(2,1)} custom-call(s32[1,192]{1,0:T(1,128)} %bitcast.9, bf16[6,16,64,256]{3,2,1,0:T(8,128)(2,1)} %pixels.1, bf16[2304,512]{1,0:T(8,128)(2,1)} %bitcast.5, f32[1,512]{1,0:T(1,128)} %bitcast.6, bf16[3,512,512]{2,1,0:T(8,128)(2,1)} %w_time.1, f32[1,512]{1,0:T(1,128)} %bitcast.7, f32[1,512]{1,0:T(1,128)} %bitcast.8), custom_call_target="tpu_custom_call" | custom-call | tf_op jit(solution)/shard_map/pallas_call | solution.py:648
  42.5 2.1 %copy.9 = bf16[24,2,16,512]{3,2,1,0:T(8,128)(2,1)} copy(bf16[24,2,16,512]{3,2,1,0:T(8,128)(2,1)} %shard_map.73) | data formatting | bytes 1572864

commit v7 on v6

--- a/solution.py
+++ b/solution.py
@@ -299,7 +299,7 @@
     (
         forward_out, packed_n, packed_f,
         in_sem, w_sem, send_n, recv_n, send_f, recv_f, send_x, recv_x,
-        send_r, send_yn, recv_yn, send_yf, recv_yf,
+        send_r, send_yn, recv_yn, send_yf, recv_yf, picked, send_out,
     ) = landing[4 * frames * pieces:]
     parts = frames * pieces
     breadth = lat.shape[-1]
@@ -410,6 +410,14 @@
                 2, frames, cap, area, breadth
             )
 
+    def store(q):
+        h = q % pieces
+        return pltpu.make_async_copy(
+            picked.at[q],
+            out.at[:, q // pieces, :, pl.ds(h * breadth, breadth)],
+            send_out.at[q],
+        )
+
     def near_copy(q, j, source):
         return pltpu.make_async_remote_copy(
             src_ref=lat.at[q % pieces, low + j, q // pieces],
@@ -555,16 +563,16 @@
         @pl.when(k == 0)
         def _():
             send_relay(0, 0)
-            send_relay(1, 0)
             send_far(0, 0)
             send_far(1, 0)
 
         @pl.when(k == 1)
         def _():
             send_relay(0, 1)
-            send_relay(1, 1)
             send_far(0, 1)
             send_far(1, 1)
+            send_relay(1, 0)
+            send_relay(1, 1)
 
         @pl.when(k == 2)
         def _():
@@ -608,8 +616,9 @@
 
         @pl.loop(0, group_tiles, unroll=4)
         def _(i):
-            h = q % pieces
-            out[i, q // pieces, :, h * breadth:(h + 1) * breadth] = rec[q][index[0, pick_at + i]]
+            picked[q, i] = rec[q][index[0, pick_at + i]]
+
+        store(q).start()
 
     for q in range(parts):
         for k in range(1, HALF):
@@ -618,6 +627,7 @@
         for j in range(HALF):
             far_copy(q, j, mine).wait_send()
         forward(q).wait_send()
+        store(q).wait()
         for k in range(1, rows):
             tile_far(q, k).wait_send()
             tile_near(q, k).wait_send()
@@ -649,7 +659,7 @@
         functools.partial(encode, rows, slabs, cap, bucket, group_tiles, pieces),
         out_shape=jax.ShapeDtypeStruct((group_tiles, frames, area, features), bf16),
         in_specs=[hbm] * 7,
-        out_specs=vmem,
+        out_specs=hbm,
         scratch_shapes=[
             pltpu.VMEM((steps, span, cap, pix_count, channels), bf16),
             pltpu.VMEM((9 * channels, features), bf16),
@@ -671,6 +681,7 @@
             dma((parts, HALF)), dma((parts, HALF)), dma((parts, HALF)), dma((parts, HALF + 1)),
             dma((parts, HALF)), dma((parts, HALF)), dma((parts,)),
             dma((parts, rows - 1)), dma((parts, rows - 1)), dma((parts, rows - 1)), dma((parts, rows - 1)),
+            held(parts, group_tiles), dma((parts,)),
         ],
         compiler_params=pltpu.CompilerParams(
             collective_id=1, has_side_effects=True, vmem_limit_bytes=62 << 20

time: 45 us -> 44.5 us (0.989)
  no operation moved by 1% of the time
where the time goes in v7:
time: 44.5 us; the launch traced here: 44.4 us
  Pallas kernels  42.3 us (95%)
  local copies, waits for them, and re-layouts  2.09 us (5%)
    pallas_call x1, Pallas kernels, body_two_blocks(): pl.pallas_call(functools.partial(encode, rows, slabs, cap, bucket, group_...  42.3 us
    unnamed x1, local copies, waits for them, and re-layouts  2.09 us

profile of v7, /device:TPU:0, one launch (start us, length us, event | category | flops | bytes accessed | tf_op | source)
XLA Modules:
  0.0 44.4 jit_solution(10177752550653160501)
XLA Ops:
  0.0 42.3 %shard_map.73 = bf16[24,2,16,512]{3,2,1,0:T(8,128)(2,1)} custom-call(s32[1,192]{1,0:T(1,128)} %bitcast.9, bf16[6,16,64,256]{3,2,1,0:T(8,128)(2,1)} %pixels.1, bf16[2304,512]{1,0:T(8,128)(2,1)} %bitcast.5, f32[1,512]{1,0:T(1,128)} %bitcast.6, bf16[3,512,512]{2,1,0:T(8,128)(2,1)} %w_time.1, f32[1,512]{1,0:T(1,128)} %bitcast.7, f32[1,512]{1,0:T(1,128)} %bitcast.8), custom_call_target="tpu_custom_call" | custom-call | tf_op jit(solution)/shard_map/pallas_call | solution.py:658
  42.3 2.1 %copy.9 = bf16[24,2,16,512]{3,2,1,0:T(8,128)(2,1)} copy(bf16[24,2,16,512]{3,2,1,0:T(8,128)(2,1)} %shard_map.73) | data formatting | bytes 1572864

commit v8 on v7

--- a/solution.py
+++ b/solution.py
@@ -577,15 +577,15 @@
         @pl.when(k == 2)
         def _():
             send_near(0, 0)
-            send_near(1, 0)
 
         @pl.when(k == 3)
         def _():
             send_near(0, 1)
-            send_near(1, 1)
             run_relay(0)
-            run_relay(1)
-
+
+    send_near(1, 0)
+    send_near(1, 1)
+    run_relay(1)
     send_near(2, 0)
     send_near(2, 1)
     send_relay(2, 0)

time: 44.5 us -> 44.5 us (level)
  no operation moved by 1% of the time
where the time goes in v8:
time: 44.5 us; the launch traced here: 44.4 us
  Pallas kernels  42.3 us (95%)
  local copies, waits for them, and re-layouts  2.09 us (5%)
    pallas_call x1, Pallas kernels, body_two_blocks(): pl.pallas_call(functools.partial(encode, rows, slabs, cap, bucket, group_...  42.3 us
    unnamed x1, local copies, waits for them, and re-layouts  2.09 us

profile of v8, /device:TPU:0, one launch (start us, length us, event | category | flops | bytes accessed | tf_op | source)
XLA Modules:
  0.0 44.4 jit_solution(5741636259279779252)
XLA Ops:
  0.0 42.3 %shard_map.73 = bf16[24,2,16,512]{3,2,1,0:T(8,128)(2,1)} custom-call(s32[1,192]{1,0:T(1,128)} %bitcast.9, bf16[6,16,64,256]{3,2,1,0:T(8,128)(2,1)} %pixels.1, bf16[2304,512]{1,0:T(8,128)(2,1)} %bitcast.5, f32[1,512]{1,0:T(1,128)} %bitcast.6, bf16[3,512,512]{2,1,0:T(8,128)(2,1)} %w_time.1, f32[1,512]{1,0:T(1,128)} %bitcast.7, f32[1,512]{1,0:T(1,128)} %bitcast.8), custom_call_target="tpu_custom_call" | custom-call | tf_op jit(solution)/shard_map/pallas_call | solution.py:658
  42.3 2.1 %copy.9 = bf16[24,2,16,512]{3,2,1,0:T(8,128)(2,1)} copy(bf16[24,2,16,512]{3,2,1,0:T(8,128)(2,1)} %shard_map.73) | data formatting | bytes 1572864
